TPU v7x, 256 devices: a whole 4x4x8 slice. The times are simulated.
256 devices in a mesh: dp: 32 (over x, y, core), owner: 8 (over z).
Axes of the slice: x: 4, y: 4, z: 8, core: 2. Of those that a mesh axis runs over, the one named last changes fastest.
Arguments:
- hidden: bfloat16 [8192, 14336], P('dp'), may hold values from -6 to 6
- grad_out: bfloat16 [8192, 4096], P('dp'), may hold values from -6 to 6
- block_row: int32 [1536], replicated, may hold values from 0 to 111
- block_col: int32 [1536], replicated, may hold values from 0 to 31
- owner_of: int32 [1536, 1], replicated, may hold values from 0 to 7; in each aligned block of 1536 rows (0 to 1535, 1536 to 3071, ...) at most 384 rows name the same one
- master: float32 [8, 384, 128, 128], P('owner', 'dp'), may hold values from -6 to 6
- moment1: float32 [8, 384, 128, 128], P('owner', 'dp'), may hold values from -0.0029296875 to 0.0029296875
- moment2: float32 [8, 384, 128, 128], P('owner', 'dp'), may hold values from 9.934108e-09 to 1.5894572e-07
Outputs:
- updated: float32 [8, 384, 128, 128], P('owner', 'dp')
Inputs may be any that keep to these rules, and one draw needn't show every extreme that they name: `owner_of`: each owner index names at most 384 listed blocks, and one of them names exactly 384.
All inputs are finite; a program needn't handle non-finite values.
Results may differ from a plain program's by a relative error of at most 0.0006.
Values may be sent and summed in bfloat16 or wider, within the bound.
A program may use at most 128 MiB of HBM per device.

v0:
```python
import functools
import math

import jax
import jax.numpy as jnp
from jax import lax
from jax.sharding import Mesh
from jax.sharding import PartitionSpec as P

BLOCK = 128
CAP = 384
DP = ("dp_0", "dp_1", "dp_2")
DP_OWNER = ("dp_0", "dp_1", "dp_2", "owner")


def by_axis(array, axes):
    return functools.reduce(lax.psum, axes, array)


def slot_table(owner_of, block_row, block_col, me_index, capacity):
    owned = (owner_of[:, 0] == me_index).astype(jnp.int32)
    ranks = jnp.cumsum(owned) - 1
    slots = jnp.arange(capacity, dtype=jnp.int32)
    match = (owned[None, :] == 1) & (ranks[None, :] == slots[:, None])
    live = jnp.any(match, axis=1).astype(jnp.float32)
    slot_rows = jnp.sum(jnp.where(match, block_row[None, :], 0), axis=1)
    slot_cols = jnp.sum(jnp.where(match, block_col[None, :], 0), axis=1)
    return (slot_rows, slot_cols, live)


def on_device(hidden, grad_out, block_row, block_col, owner_of, master, moment1, moment2):
    tokens_here = hidden.shape[0]
    share = master.shape[1]
    me_index = lax.axis_index("owner")
    slot_rows, slot_cols, live = slot_table(owner_of, block_row, block_col, me_index, CAP)
    hidden_three = hidden.reshape(tokens_here, -1, BLOCK)
    grad_three = grad_out.reshape(tokens_here, -1, BLOCK)
    group = math.gcd(share * lax.axis_size(DP), 64)

    def one_group(triple):
        row_ids, col_ids, alive = triple
        left = jnp.take(hidden_three, row_ids, axis=1)
        right = jnp.take(grad_three, col_ids, axis=1)
        product = jnp.einsum("tgi,tgj->gij", left, right, preferred_element_type=jnp.float32)
        return product * alive[:, None, None]

    blocks = lax.map(
        one_group,
        (slot_rows.reshape(-1, group), slot_cols.reshape(-1, group), live.reshape(-1, group)),
    )
    shares = lax.psum_scatter(
        blocks.reshape(share * lax.axis_size(DP), BLOCK, BLOCK).astype(jnp.bfloat16),
        DP,
        scatter_dimension=0,
        tiled=True,
    ).astype(jnp.float32)
    total = by_axis(jnp.sum(shares * shares), DP_OWNER)
    clip = 1.0 / jnp.maximum(jnp.sqrt(total), 1.0)
    scaled = clip * shares[None]
    first = 0.9 * moment1 + 0.1 * scaled
    second = 0.95 * moment2 + 0.05 * scaled * scaled
    direction = first / (1.0 - 0.9**10) / (jnp.sqrt(second / (1.0 - 0.95**10)) + 1e-08)
    return master - 0.25 * (direction + 0.1 * master)


def solution(mesh):
    finer = Mesh(
        mesh.devices.reshape(4, 4, 2, mesh.shape["owner"]), ("dp_0", "dp_1", "dp_2", "owner")
    )
    placed = (
        P(DP, None),
        P(DP, None),
        P(),
        P(),
        P(),
        P("owner", DP, None, None),
        P("owner", DP, None, None),
        P("owner", DP, None, None),
    )
    return jax.shard_map(
        on_device,
        mesh=finer,
        in_specs=placed,
        out_specs=P("owner", DP, None, None),
        check_vma=False,
    )
```

profile of v0, /device:TPU:1, one launch (start us, length us, event | category | flops | bytes accessed | tf_op | source)
XLA Modules:
  0.0 299.5 jit_solution(17070698080171383891)
XLA Ops:
  10.8 10.3 %copy.18 = bf16[256,14336]{0,1:T(8,128)(2,1)} copy(bf16[256,14336]{1,0:T(8,128)(2,1)} %param.10) | data formatting | bytes 14680064 | tf_op args[0]
  21.1 10.5 %copy.20 = bf16[256,112,128]{2,0,1:T(8,128)(2,1)} copy(bf16[256,112,128]{0,2,1:T(8,128)(2,1)} %bitcast.72) | data formatting | bytes 14680064 | tf_op jit(solution)/shard_map/while | solution.py:47
  34.2 3.2 %copy.21 = bf16[256,32,128]{2,0,1:T(8,128)(2,1)S(1)} copy(bf16[256,32,128]{0,2,1:T(8,128)(2,1)} %bitcast.74) | data formatting | bytes 4194304 | tf_op jit(solution)/shard_map/while | solution.py:47
  37.4 96.5 %while.10 = (s32[]{:T(128)}, bf16[6,64,128,128]{3,2,1,0:T(8,128)(2,1)}, s32[6,64]{1,0:T(8,128)S(1)}, bf16[256,112,128]{2,0,1:T(8,128)(2,1)}, s32[6,64]{1,0:T(8,1...) while((s32[]{:T(128)}, bf16[6,64,128,128]{3,2,1,0:T(8,128)(2,1)}, ...), condition=%wide.region_6.7_spmd, body=%wide.region_5.6_spmd.sunk | while | flops 542116992 | bytes 29372512 | solution.py:47
  37.4 3.1 %gather_fusion = bf16[64,256,128]{2,1,0:T(8,128)(2,1)} fusion(bf16[256,32,128]{2,0,1:T(8,128)(2,1)S(1)} %get-tuple-element.149, s32[1024]{0:T(1024)S(1)} %pad_clamp_fusion.4), kind=kCustom, calls=%fused_computation.1.clone.1 | custom fusion | bytes 8388864 | tf_op jit(solution)/shard_map/while/body/eval_jaxpr/jit(_take)/gather | solution.py:43
  40.5 6.3 %gather_fusion.1 = bf16[64,256,128]{2,1,0:T(8,128)(2,1)} fusion(bf16[256,112,128]{2,0,1:T(8,128)(2,1)} %get-tuple-element.147, s32[1024]{0:T(1024)S(1)} %pad_clamp_fusion.5), kind=kCustom, calls=%fused_computation.clone.1 | custom fusion | bytes 8388864 | tf_op jit(solution)/shard_map/while/body/eval_jaxpr/jit(_take)/gather | solution.py:42
  46.8 6.7 %bitcast_dynamic-update-slice_fusion.2 = bf16[6,64,128,128]{3,2,1,0:T(8,128)(2,1)} fusion(bf16[6,64,128,128]{3,2,1,0:T(8,128)(2,1)} %get-tuple-element.137, s32[]{:T(128)} %get-tuple-element.136, f32[64]{0:T(128)S(1)} %fusion.37, bf16[64,256,128]{2,1,0:T(8,128)(2,1)} %gather_fusion, pred[64]{0:T(512)(128)(4,1)S(1)} %get-tuple-element.125, ...), kind=kOutput, calls=%fused_computation.2.clone.1 | convolution fusion | flops 542113792 | bytes 12583808 | tf_op jit(solution)/shard_map/while/body/eval_jaxpr/tgi,tgj->gij/dot_general | solution.py:44
  53.5 3.1 %gather_fusion = bf16[64,256,128]{2,1,0:T(8,128)(2,1)} fusion(bf16[256,32,128]{2,0,1:T(8,128)(2,1)S(1)} %get-tuple-element.149, s32[1024]{0:T(1024)S(1)} %pad_clamp_fusion.4), kind=kCustom, calls=%fused_computation.1.clone.1 | custom fusion | bytes 8388864 | tf_op jit(solution)/shard_map/while/body/eval_jaxpr/jit(_take)/gather | solution.py:43
  56.6 6.3 %gather_fusion.1 = bf16[64,256,128]{2,1,0:T(8,128)(2,1)} fusion(bf16[256,112,128]{2,0,1:T(8,128)(2,1)} %get-tuple-element.147, s32[1024]{0:T(1024)S(1)} %pad_clamp_fusion.5), kind=kCustom, calls=%fused_computation.clone.1 | custom fusion | bytes 8388864 | tf_op jit(solution)/shard_map/while/body/eval_jaxpr/jit(_take)/gather | solution.py:42
  62.9 6.6 %bitcast_dynamic-update-slice_fusion.2 = bf16[6,64,128,128]{3,2,1,0:T(8,128)(2,1)} fusion(bf16[6,64,128,128]{3,2,1,0:T(8,128)(2,1)} %get-tuple-element.137, s32[]{:T(128)} %get-tuple-element.136, f32[64]{0:T(128)S(1)} %fusion.37, bf16[64,256,128]{2,1,0:T(8,128)(2,1)} %gather_fusion, pred[64]{0:T(512)(128)(4,1)S(1)} %get-tuple-element.125, ...), kind=kOutput, calls=%fused_computation.2.clone.1 | convolution fusion | flops 542113792 | bytes 12583808 | tf_op jit(solution)/shard_map/while/body/eval_jaxpr/tgi,tgj->gij/dot_general | solution.py:44
  69.6 3.1 %gather_fusion = bf16[64,256,128]{2,1,0:T(8,128)(2,1)} fusion(bf16[256,32,128]{2,0,1:T(8,128)(2,1)S(1)} %get-tuple-element.149, s32[1024]{0:T(1024)S(1)} %pad_clamp_fusion.4), kind=kCustom, calls=%fused_computation.1.clone.1 | custom fusion | bytes 8388864 | tf_op jit(solution)/shard_map/while/body/eval_jaxpr/jit(_take)/gather | solution.py:43
  72.7 6.3 %gather_fusion.1 = bf16[64,256,128]{2,1,0:T(8,128)(2,1)} fusion(bf16[256,112,128]{2,0,1:T(8,128)(2,1)} %get-tuple-element.147, s32[1024]{0:T(1024)S(1)} %pad_clamp_fusion.5), kind=kCustom, calls=%fused_computation.clone.1 | custom fusion | bytes 8388864 | tf_op jit(solution)/shard_map/while/body/eval_jaxpr/jit(_take)/gather | solution.py:42
  78.9 6.7 %bitcast_dynamic-update-slice_fusion.2 = bf16[6,64,128,128]{3,2,1,0:T(8,128)(2,1)} fusion(bf16[6,64,128,128]{3,2,1,0:T(8,128)(2,1)} %get-tuple-element.137, s32[]{:T(128)} %get-tuple-element.136, f32[64]{0:T(128)S(1)} %fusion.37, bf16[64,256,128]{2,1,0:T(8,128)(2,1)} %gather_fusion, pred[64]{0:T(512)(128)(4,1)S(1)} %get-tuple-element.125, ...), kind=kOutput, calls=%fused_computation.2.clone.1 | convolution fusion | flops 542113792 | bytes 12583808 | tf_op jit(solution)/shard_map/while/body/eval_jaxpr/tgi,tgj->gij/dot_general | solution.py:44
  88.7 6.3 %gather_fusion.1 = bf16[64,256,128]{2,1,0:T(8,128)(2,1)} fusion(bf16[256,112,128]{2,0,1:T(8,128)(2,1)} %get-tuple-element.147, s32[1024]{0:T(1024)S(1)} %pad_clamp_fusion.5), kind=kCustom, calls=%fused_computation.clone.1 | custom fusion | bytes 8388864 | tf_op jit(solution)/shard_map/while/body/eval_jaxpr/jit(_take)/gather | solution.py:42
  95.0 6.7 %bitcast_dynamic-update-slice_fusion.2 = bf16[6,64,128,128]{3,2,1,0:T(8,128)(2,1)} fusion(bf16[6,64,128,128]{3,2,1,0:T(8,128)(2,1)} %get-tuple-element.137, s32[]{:T(128)} %get-tuple-element.136, f32[64]{0:T(128)S(1)} %fusion.37, bf16[64,256,128]{2,1,0:T(8,128)(2,1)} %gather_fusion, pred[64]{0:T(512)(128)(4,1)S(1)} %get-tuple-element.125, ...), kind=kOutput, calls=%fused_computation.2.clone.1 | convolution fusion | flops 542113792 | bytes 12583808 | tf_op jit(solution)/shard_map/while/body/eval_jaxpr/tgi,tgj->gij/dot_general | solution.py:44
  104.8 6.3 %gather_fusion.1 = bf16[64,256,128]{2,1,0:T(8,128)(2,1)} fusion(bf16[256,112,128]{2,0,1:T(8,128)(2,1)} %get-tuple-element.147, s32[1024]{0:T(1024)S(1)} %pad_clamp_fusion.5), kind=kCustom, calls=%fused_computation.clone.1 | custom fusion | bytes 8388864 | tf_op jit(solution)/shard_map/while/body/eval_jaxpr/jit(_take)/gather | solution.py:42
  111.1 6.7 %bitcast_dynamic-update-slice_fusion.2 = bf16[6,64,128,128]{3,2,1,0:T(8,128)(2,1)} fusion(bf16[6,64,128,128]{3,2,1,0:T(8,128)(2,1)} %get-tuple-element.137, s32[]{:T(128)} %get-tuple-element.136, f32[64]{0:T(128)S(1)} %fusion.37, bf16[64,256,128]{2,1,0:T(8,128)(2,1)} %gather_fusion, pred[64]{0:T(512)(128)(4,1)S(1)} %get-tuple-element.125, ...), kind=kOutput, calls=%fused_computation.2.clone.1 | convolution fusion | flops 542113792 | bytes 12583808 | tf_op jit(solution)/shard_map/while/body/eval_jaxpr/tgi,tgj->gij/dot_general | solution.py:44
  121.0 6.3 %gather_fusion.1 = bf16[64,256,128]{2,1,0:T(8,128)(2,1)} fusion(bf16[256,112,128]{2,0,1:T(8,128)(2,1)} %get-tuple-element.147, s32[1024]{0:T(1024)S(1)} %pad_clamp_fusion.5), kind=kCustom, calls=%fused_computation.clone.1 | custom fusion | bytes 8388864 | tf_op jit(solution)/shard_map/while/body/eval_jaxpr/jit(_take)/gather | solution.py:42
  127.2 6.6 %bitcast_dynamic-update-slice_fusion.2 = bf16[6,64,128,128]{3,2,1,0:T(8,128)(2,1)} fusion(bf16[6,64,128,128]{3,2,1,0:T(8,128)(2,1)} %get-tuple-element.137, s32[]{:T(128)} %get-tuple-element.136, f32[64]{0:T(128)S(1)} %fusion.37, bf16[64,256,128]{2,1,0:T(8,128)(2,1)} %gather_fusion, pred[64]{0:T(512)(128)(4,1)S(1)} %get-tuple-element.125, ...), kind=kOutput, calls=%fused_computation.2.clone.1 | convolution fusion | flops 542113792 | bytes 12583808 | tf_op jit(solution)/shard_map/while/body/eval_jaxpr/tgi,tgj->gij/dot_general | solution.py:44
  133.9 113.9 %reduce-scatter.2.cloned.1.call-done = bf16[12,128,128]{2,1,0:T(8,128)(2,1)} async-done(((bf16[384,128,128]{2,1,0:T(8,128)(2,1)}), bf16[12,128,128]{2,1,0:T(8,128)(2,1)}) %reduce-scatter.2.cloned.1.call-update) | async-done | bytes 393232 | tf_op jit(solution)/shard_map/reduce_scatter | solution.py:51
  249.7 8.8 %psum.28 = f32[]{:T(128)} all-reduce(f32[]{:T(128)} %fusion.24), channel_id=1, replica_groups=mesh['dp_0'=4,'dp_1'=4,'dp_2'=2,'owner'=8] {'dp_0'}, use_global_device_ids=true, to_apply=%region_9.10 | all-reduce | flops 1 | bytes 8 | tf_op jit(solution)/shard_map/psum | solution.py:17
  258.4 7.2 %psum.29 = f32[]{:T(128)} all-reduce(f32[]{:T(128)} %psum.28), channel_id=1, replica_groups=mesh['dp_0'=4,'dp_1'=4,'dp_2'=2,'owner'=8] {'dp_1'}, use_global_device_ids=true, to_apply=%region_10.11 | all-reduce | flops 1 | bytes 8 | tf_op jit(solution)/shard_map/psum | solution.py:17
  265.7 9.0 %psum.30 = f32[]{:T(128)} all-reduce(f32[]{:T(128)} %psum.29), channel_id=1, replica_groups=mesh['dp_0'=4,'dp_1'=4,'dp_2'=2,'owner'=8] {'dp_2'}, use_global_device_ids=true, to_apply=%region_11.12 | all-reduce | flops 1 | bytes 8 | tf_op jit(solution)/shard_map/psum | solution.py:17
  274.7 14.6 %psum.31 = f32[]{:T(128)} all-reduce(f32[]{:T(128)} %psum.30), channel_id=1, replica_groups=mesh['dp_0'=4,'dp_1'=4,'dp_2'=2,'owner'=8] {'owner'}, use_global_device_ids=true, to_apply=%region_12.13 | all-reduce | flops 1 | bytes 8 | tf_op jit(solution)/shard_map/psum | solution.py:17
  (60 shorter events, 20.6 us)
Async XLA Ops:
  6.5 241.3 %reduce-scatter.2.cloned.1.call-start = ((), (), s32[]{:S(2)}) async-start(), calls=%async_computation.1 | async-start | bytes 12976128 | tf_op jit(solution)/shard_map/reduce_scatter | solution.py:51
  21.1 10.5 %copy-start = (bf16[256,4096]{1,0:T(8,128)(2,1)S(1)}, bf16[256,4096]{1,0:T(8,128)(2,1)}, u32[]{:S(2)}) copy-start(bf16[256,4096]{1,0:T(8,128)(2,1)} %param.11) | copy-start | bytes 6291460
  133.9 156.2 %copy-start.1 = (f32[1,12,128,128]{3,2,1,0:T(8,128)S(1)}, f32[1,12,128,128]{3,2,1,0:T(8,128)}, u32[]{:S(2)}) copy-start(f32[1,12,128,128]{3,2,1,0:T(8,128)} %param.15) | copy-start | bytes 2359300
  133.9 156.2 %copy-start.2 = (f32[1,12,128,128]{3,2,1,0:T(8,128)S(1)}, f32[1,12,128,128]{3,2,1,0:T(8,128)}, u32[]{:S(2)}) copy-start(f32[1,12,128,128]{3,2,1,0:T(8,128)} %param.17) | copy-start | bytes 2359300
  133.9 156.2 %copy-start.3 = (f32[1,12,128,128]{3,2,1,0:T(8,128)S(1)}, f32[1,12,128,128]{3,2,1,0:T(8,128)}, u32[]{:S(2)}) copy-start(f32[1,12,128,128]{3,2,1,0:T(8,128)} %param.16) | copy-start | bytes 2359300
Sparse Core Ops, SparseCore 0:
  134.0 113.7 reduce-scatter.1
where the time goes:
time: 303 us; the launch traced here: 299 us
  waiting for transfers between devices  114 us (38%)
  local copies, waits for them, and re-layouts  83.1 us (27%)
  matrix products  40.1 us (13%)
  blocking collectives  39.7 us (13%)
  between operations  14.2 us (5%)
  other arithmetic  8.36 us (3%)
    reduce_scatter x1, waiting for transfers between devices, on_device(): lax.psum_scatter(blocks.reshape(share * lax.axis_size(DP), BLOCK, BLOCK)....  114 us
    dot_general x6, matrix products, one_group(): jnp.einsum('tgi,tgj->gij', left, right, preferred_element_type=jnp.float32)  40.1 us
    psum x4, blocking collectives, by_axis(): return functools.reduce(lax.psum, axes, array)  39.7 us
    gather x6, local copies, waits for them, and re-layouts, one_group(): left = jnp.take(hidden_three, row_ids, axis=1)  37.5 us
    gather x6, local copies, waits for them, and re-layouts, one_group(): right = jnp.take(grad_three, col_ids, axis=1)  18.6 us
    while x2, local copies, waits for them, and re-layouts, on_device(): lax.map(one_group, (slot_rows.reshape(-1, group), slot_cols.reshape(-1, g...  13.8 us
    unnamed x10, local copies, waits for them, and re-layouts  12.8 us
  transfers between devices with their start and end apart: 1, of which 1 were waited for; matrix products, arithmetic and copies ran while one was open for 0% of the time, Pallas kernels for 0%

commit v1 on v0

v1 whole, which is shorter than its diff:
```python
import functools

import jax
import jax.numpy as jnp
from jax import lax
from jax.experimental import pallas as pl
from jax.experimental.pallas import tpu as pltpu
from jax.sharding import PartitionSpec as P

BLOCK = 128
CAP = 384
N_OWNER = 8
MESH = pl.DeviceIdType.MESH
PAIR, XA, XB0, XB1, YA, YB0, YB1 = 0, 1, 3, 5, 7, 9, 11


def slot_table(owner_of, block_row, block_col, me_index, capacity):
    owned = (owner_of[:, 0] == me_index).astype(jnp.int32)
    ranks = jnp.cumsum(owned) - 1
    slots = jnp.arange(capacity, dtype=jnp.int32)
    match = (owned[None, :] == 1) & (ranks[None, :] == slots[:, None])
    live = jnp.any(match, axis=1).astype(jnp.float32)
    slot_rows = jnp.sum(jnp.where(match, block_row[None, :], 0), axis=1)
    slot_cols = jnp.sum(jnp.where(match, block_col[None, :], 0), axis=1)
    return (slot_rows, slot_cols, live)


def wrap(value, size):
    return lax.rem(value, size)


def kernel(items, row_ref, col_ref, live_ref, hidden_hbm, grad_hbm, slot_grad_ref, total_ref,
           hidden, grad, grad_t, to_pair, from_pair, chip, ring_a, ring_b, line, last_a, last_b,
           sums, sum_in, load_sem, send_sem, recv_sem, sum_send, sum_recv):
    f32, bf16 = jnp.float32, jnp.bfloat16
    d = lax.axis_index("dp")
    z = lax.axis_index("owner")
    x, y, c = lax.div(d, 8), wrap(lax.div(d, 2), 4), wrap(d, 2)

    def device(px, py, pc):
        return {"dp": (px * 4 + py) * 2 + pc}

    partner = device(x, y, 1 - c)

    def near(axis, step):
        if axis == 0:
            return device(wrap(x + step, 4), y, c)
        return device(x, wrap(y + step, 4), c)

    def up(step):
        return {"owner": wrap(z + step, N_OWNER)}

    def load(src, dst, sem):
        def body(k, carry):
            columns = pl.ds(pl.multiple_of(k * BLOCK, BLOCK), BLOCK)
            pltpu.make_async_copy(src.at[:, columns], dst.at[k], sem).start()
            return carry
        lax.fori_loop(0, dst.shape[0], body, 0)

    load(grad_hbm, grad, load_sem.at[0])
    load(hidden_hbm, hidden, load_sem.at[1])

    groups = [[partner], [near(0, k) for k in (1, 2, 3)], [near(1, k) for k in (1, 2, 3)],
              [up(k) for k in range(1, N_OWNER)]]
    barrier = pltpu.get_barrier_semaphore()
    everyone = [who for group in groups for who in group]
    for who in everyone:
        pl.semaphore_signal(barrier, inc=1, device_id=who, device_id_type=MESH)

    pltpu.make_async_copy(grad, grad, load_sem.at[0]).wait()

    def turn(k, carry):
        grad_t[k] = grad[k].T
        return carry

    lax.fori_loop(0, grad_t.shape[0], turn, 0)
    pltpu.make_async_copy(hidden, hidden, load_sem.at[1]).wait()
    pl.semaphore_wait(barrier, len(everyone))

    started = []

    def send(src, dst, item, kind, who):
        copy = pltpu.make_async_remote_copy(
            src_ref=src, dst_ref=dst, send_sem=send_sem.at[item, kind],
            recv_sem=recv_sem.at[item, kind], device_id=who, device_id_type=MESH)
        copy.start()
        started.append(copy)
        arrivals[item, kind] = copy

    arrivals = {}

    def arrive(item, kind):
        arrivals[item, kind].wait_recv()

    def product(slot):
        row, col = row_ref[slot], col_ref[slot]
        return jnp.dot(grad_t[col], hidden[row], preferred_element_type=f32)

    def slot_of(item, ra, rb, core):
        if item % 2 == 0:
            px, py = wrap(x + ra, 4), wrap(y + rb, 4)
        else:
            px, py = wrap(x + rb, 4), wrap(y + ra, 4)
        return ((px * 4 + py) * 2 + core) * items + item

    def partner_products(item):
        def body(ra, carry):
            for rb in range(4):
                to_pair[item, ra * 4 + rb] = product(slot_of(item, ra, rb, 1 - c)).astype(bf16)
            return carry
        lax.fori_loop(0, 4, body, 0)
        send(to_pair.at[item], from_pair.at[item], item, PAIR, partner)

    def own_products(item):
        arrive(item, PAIR)

        def body(ra, carry):
            for rb in range(4):
                j = ra * 4 + rb
                value = product(slot_of(item, ra, rb, c)) + from_pair[item, j].astype(f32)
                chip[item, j] = value.astype(bf16)
            return carry
        lax.fori_loop(0, 4, body, 0)
        axis = item % 2
        send(chip.at[item, pl.ds(8, 2)], ring_a.at[item, 0], item, XA, near(axis, 1))
        send(chip.at[item, pl.ds(10, 2)], ring_a.at[item, 1], item, XA + 1, near(axis, 3))
        send(chip.at[item, pl.ds(6, 2)], ring_b.at[item, 0, pl.ds(2, 2)], item, XB0, near(axis, 1))
        send(chip.at[item, pl.ds(12, 2)], ring_b.at[item, 1, pl.ds(0, 2)], item, XB0 + 1, near(axis, 3))

    def ring_step(item):
        axis = item % 2
        arrive(item, XA)
        chip[item, 4:6] = (chip[item, 4:6].astype(f32) + ring_a[item, 0].astype(f32)).astype(bf16)
        send(chip.at[item, pl.ds(4, 2)], ring_b.at[item, 0, pl.ds(0, 2)], item, XB1, near(axis, 1))
        arrive(item, XA + 1)
        chip[item, 14:16] = (chip[item, 14:16].astype(f32) + ring_a[item, 1].astype(f32)).astype(bf16)
        send(chip.at[item, pl.ds(14, 2)], ring_b.at[item, 1, pl.ds(2, 2)], item, XB1 + 1, near(axis, 3))

    def ring_end(item):
        axis = 1 - item % 2
        for kind in (XB0, XB0 + 1, XB1, XB1 + 1):
            arrive(item, kind)
        for rb in (2, 1, 3, 0):
            value = (chip[item, rb].astype(f32) + ring_b[item, 0, rb].astype(f32)
                     + ring_b[item, 1, rb].astype(f32))
            line[item, rb] = value.astype(bf16)
        half = BLOCK // 2
        low, high = pl.ds(0, half), pl.ds(half, half)
        send(line.at[item, 2, low], last_a.at[item, 0], item, YA, near(axis, 1))
        send(line.at[item, 2, high], last_a.at[item, 1], item, YA + 1, near(axis, 3))
        send(line.at[item, 1, high], last_b.at[item, 0, high], item, YB0, near(axis, 1))
        send(line.at[item, 3, low], last_b.at[item, 1, low], item, YB0 + 1, near(axis, 3))

    def line_step(item):
        axis = 1 - item % 2
        half = BLOCK // 2
        low, high = pl.ds(0, half), pl.ds(half, half)
        arrive(item, YA)
        line[item, 1, :half] = (line[item, 1, :half].astype(f32) + last_a[item, 0].astype(f32)).astype(bf16)
        send(line.at[item, 1, low], last_b.at[item, 0, low], item, YB1, near(axis, 1))
        arrive(item, YA + 1)
        line[item, 3, half:] = (line[item, 3, half:].astype(f32) + last_a[item, 1].astype(f32)).astype(bf16)
        send(line.at[item, 3, high], last_b.at[item, 1, high], item, YB1 + 1, near(axis, 3))

    def finish(item):
        for kind in (YB0, YB0 + 1, YB1, YB1 + 1):
            arrive(item, kind)
        value = (line[item, 0].astype(f32) + last_b[item, 0].astype(f32) + last_b[item, 1].astype(f32))
        value = value * live_ref[d * items + item]
        slot_grad_ref[item] = value.T
        return jnp.sum((value * value).reshape(-1, 8, BLOCK), axis=0)

    steps = items // 2
    part = jnp.zeros((8, BLOCK), f32)
    both = lambda stage, step: [stage(2 * step + q) for q in (0, 1)] if 0 <= step < steps else []
    for tick in range(-1, steps + 4):
        both(partner_products, tick + 1)
        both(own_products, tick)
        both(ring_step, tick - 1)
        both(line_step, tick - 3)
        both(ring_end, tick - 2)
        for piece in both(finish, tick - 4):
            part = part + piece

    sums[0] = part
    first = 0
    for n, group in enumerate(groups):
        for k, who in enumerate(group):
            copy = pltpu.make_async_remote_copy(
                src_ref=sums.at[n], dst_ref=sum_in.at[first + k], send_sem=sum_send.at[first + k],
                recv_sem=sum_recv.at[first + k], device_id=who, device_id_type=MESH)
            copy.start()
            started.append(copy)
        for k, copy in enumerate(started[-len(group):]):
            copy.wait_recv()
            part = part + sum_in[first + k]
        first += len(group)
        if n + 1 < len(groups):
            sums[n + 1] = part
    total_ref[...] = part
    for copy in started:
        copy.wait_send()


def reduce_blocks(rows, cols, live, hidden, grad_out, items):
    tokens, features = hidden.shape[0], grad_out.shape[1]
    bf16, f32 = jnp.bfloat16, jnp.float32
    peers = 1 + 3 + 3 + N_OWNER - 1
    block = (BLOCK, BLOCK)
    smem = pl.BlockSpec(memory_space=pltpu.SMEM)
    vmem = pl.BlockSpec(memory_space=pltpu.VMEM)
    hbm = pl.BlockSpec(memory_space=pl.ANY)
    return pl.pallas_call(
        functools.partial(kernel, items),
        out_shape=(jax.ShapeDtypeStruct((items, *block), f32), jax.ShapeDtypeStruct((8, BLOCK), f32)),
        in_specs=[smem, smem, smem, hbm, hbm],
        out_specs=(vmem, vmem),
        scratch_shapes=[
            pltpu.VMEM((hidden.shape[1] // BLOCK, tokens, BLOCK), bf16),
            pltpu.VMEM((features // BLOCK, tokens, BLOCK), bf16),
            pltpu.VMEM((features // BLOCK, BLOCK, tokens), bf16),
            pltpu.VMEM((items, 16, *block), bf16),
            pltpu.VMEM((items, 16, *block), bf16),
            pltpu.VMEM((items, 16, *block), bf16),
            pltpu.VMEM((items, 2, 2, *block), bf16),
            pltpu.VMEM((items, 2, 4, *block), bf16),
            pltpu.VMEM((items, 4, *block), bf16),
            pltpu.VMEM((items, 2, BLOCK // 2, BLOCK), bf16),
            pltpu.VMEM((items, 2, *block), bf16),
            pltpu.VMEM((4, 8, BLOCK), f32),
            pltpu.VMEM((peers, 8, BLOCK), f32),
            pltpu.SemaphoreType.DMA((2,)),
            pltpu.SemaphoreType.DMA((items, 13)),
            pltpu.SemaphoreType.DMA((items, 13)),
            pltpu.SemaphoreType.DMA((peers,)),
            pltpu.SemaphoreType.DMA((peers,)),
        ],
        compiler_params=pltpu.CompilerParams(
            collective_id=0, has_side_effects=True, vmem_limit_bytes=62 * 1024 * 1024),
        name="reduce_blocks",
    )(rows, cols, live, hidden, grad_out)


def on_device(hidden, grad_out, block_row, block_col, owner_of, master, moment1, moment2):
    share = master.shape[1]
    me_index = lax.axis_index("owner")
    rows, cols, live = slot_table(owner_of, block_row, block_col, me_index, CAP)
    shares, parts = reduce_blocks(rows, cols, live, hidden, grad_out, share)
    total = jnp.sum(parts)
    clip = 1.0 / jnp.maximum(jnp.sqrt(total), 1.0)
    scaled = clip * shares[None]
    first = 0.9 * moment1 + 0.1 * scaled
    second = 0.95 * moment2 + 0.05 * scaled * scaled
    direction = first / (1.0 - 0.9**10) / (jnp.sqrt(second / (1.0 - 0.95**10)) + 1e-08)
    return master - 0.25 * (direction + 0.1 * master)


def solution(mesh):
    placed = (
        P("dp", None),
        P("dp", None),
        P(),
        P(),
        P(),
        P("owner", "dp", None, None),
        P("owner", "dp", None, None),
        P("owner", "dp", None, None),
    )
    return jax.shard_map(
        on_device,
        mesh=mesh,
        in_specs=placed,
        out_specs=P("owner", "dp", None, None),
        check_vma=False,
    )
```

time: 303 us -> 85.3 us (0.28); the launches traced: 299 us -> 84.9 us
  waiting for transfers between devices: 114 us -> 0 us
  local copies, waits for them, and re-layouts: 83.1 us -> 0.2 us
  Pallas kernels: 0 us -> 74.8 us
  matrix products: 40.1 us -> 0 us
  blocking collectives: 39.7 us -> 0 us
  between operations: 14.2 us -> 0.77 us
    reduce_scatter x1 -> x0, waiting for transfers between devices: 114 us -> none  [on_device(): lax.psum_scatter(blocks.reshape(share * lax.axis_size(DP), BLOCK, BLOCK)....]
    pallas_call x0 -> x1, Pallas kernels: none -> 74.8 us  [reduce_blocks(): pl.pallas_call(functools.partial(kernel, items), out_shape=(jax.ShapeDtyp...]
    gather x12 -> x0, local copies, waits for them, and re-layouts: 56.1 us -> none  [the longest x6 37.5 us: one_group(): left = jnp.take(hidden_three, row_ids, axis=1)]
    dot_general x6 -> x0, matrix products: 40.1 us -> none  [one_group(): jnp.einsum('tgi,tgj->gij', left, right, preferred_element_type=jnp.float32)]
    psum x4 -> x0, blocking collectives: 39.7 us -> none  [by_axis(): return functools.reduce(lax.psum, axes, array)]
    while x2 -> x0, local copies, waits for them, and re-layouts: 13.8 us -> none  [on_device(): lax.map(one_group, (slot_rows.reshape(-1, group), slot_cols.reshape(-1, g...]
    unnamed x10 -> x4, local copies, waits for them, and re-layouts: 12.8 us -> 0.01 us
  transfers between devices with their start and end apart: 1 -> 0, of which waited for: 1 -> 0; matrix products, arithmetic and copies ran while one was open for 0% -> 0% of each run, Pallas kernels for 0% -> 0%
where the time goes in v1:
time: 85.3 us; the launch traced here: 84.9 us
  Pallas kernels  74.8 us (88%)
  other arithmetic  9.15 us (11%)
    pallas_call x1, Pallas kernels, reduce_blocks(): pl.pallas_call(functools.partial(kernel, items), out_shape=(jax.ShapeDtyp...  74.8 us
    sub x1, other arithmetic, on_device(): return master - 0.25 * (direction + 0.1 * master)  2.87 us
    reduce_sum x1, other arithmetic, slot_table(): slot_cols = jnp.sum(jnp.where(match, block_col[None, :], 0), axis=1)  2.21 us

profile of v1, /device:TPU:1, one launch (start us, length us, event | category | flops | bytes accessed | tf_op | source)
XLA Modules:
  0.0 84.9 jit_solution(13357397754990688762)
XLA Ops:
  0.0 0.7 compare_reduce_fusion
  0.7 0.7 fusion.10
  1.4 0.3 reduce-window.9
  1.7 0.1 slice.9
  1.8 0.1 slice_reduce_fusion
  1.9 0.1 add_bitcast_fusion
  2.0 0.4 fusion.1
  2.4 2.2 %select_reduce_fusion = (s32[384]{0:T(512)}, s32[384]{0:T(512)}) fusion(s32[1536]{0:T(1024)} %param.11, s32[1536]{0:T(1024)S(1)} %add_bitcast_fusion, pred[1536]{0:T(1024)(128)(4,1)S(1)} %compare_reduce_fusion, s32[1536]{0:T(1024)} %param.10), kind=kLoop, calls=%fused_computation | loop fusion | flops 3538176 | bytes 23040 | tf_op jit(solution)/shard_map/reduce_sum | solution.py:24
  4.6 0.6 convert_element_type.20.live_ref
  5.2 0.0 copy-start
  5.2 0.0 copy-start.1
  5.2 74.8 %reduce_blocks.1 = (f32[12,128,128]{2,1,0:T(8,128)}, f32[8,128]{1,0:T(8,128)}) custom-call(s32[384]{0:T(512)} %get-tuple-element.10.row_ref, s32[384]{0:T(512)} %get-tuple-element.9.col_ref, f32[384]{0:T(512)} %convert_element_type.20.live_ref, bf16[256,14336]{1,0:T(8,128)(2,1)} %hidden_hbm.1, bf16[256,4096]{1,0:T(8,128)(2,1)} %grad_hbm.1), custom_call_target="tpu_custom_call" | custom-call | tf_op jit(solution)/shard_map/reduce_blocks/pallas_call | solution.py:213
  80.0 1.3 %reduce_sum.29 = f32[]{:T(128)} reduce(f32[8,128]{1,0:T(8,128)} %get-tuple-element.7, f32[]{:T(128)} %constant.11.clone.1), dimensions={0,1}, to_apply=%region_5.6 | reduce | flops 1023 | bytes 4104 | tf_op jit(solution)/shard_map/reduce_sum | solution.py:249
  82.0 0.0 copy-done
  82.0 0.0 copy-done.1
  82.1 2.9 %multiply_subtract_fusion = f32[1,12,128,128]{3,2,1,0:T(8,128)} fusion(f32[1,12,128,128]{3,2,1,0:T(8,128)S(1)} %copy-done, f32[1,12,128,128]{3,2,1,0:T(8,128)S(1)} %copy-done.1, f32[12,128,128]{2,1,0:T(8,128)} %get-tuple-element.8, f32[1,12,128,128]{3,2,1,0:T(8,128)} %param.14, f32[]{:T(128)S(6)} %div.18), kind=kLoop, calls=%fused_computation.15 | loop fusion | flops 3145728 | bytes 3932164 | tf_op jit(solution)/shard_map/sub | solution.py:255
  (1 shorter events, 0.0 us)
Async XLA Ops:
  5.2 76.8 %copy-start = (f32[1,12,128,128]{3,2,1,0:T(8,128)S(1)}, f32[1,12,128,128]{3,2,1,0:T(8,128)}, u32[]{:S(2)}) copy-start(f32[1,12,128,128]{3,2,1,0:T(8,128)} %param.13) | copy-start | bytes 2359300
  5.2 76.8 %copy-start.1 = (f32[1,12,128,128]{3,2,1,0:T(8,128)S(1)}, f32[1,12,128,128]{3,2,1,0:T(8,128)}, u32[]{:S(2)}) copy-start(f32[1,12,128,128]{3,2,1,0:T(8,128)} %param.15) | copy-start | bytes 2359300

commit v2 on v1

--- a/solution.py
+++ b/solution.py
@@ -8,30 +8,36 @@
 from jax.sharding import PartitionSpec as P
 
 BLOCK = 128
-CAP = 384
 N_OWNER = 8
 MESH = pl.DeviceIdType.MESH
+CHUNKS = 3
+CHIPS = 16
 PAIR, XA, XB0, XB1, YA, YB0, YB1 = 0, 1, 3, 5, 7, 9, 11
 
 
-def slot_table(owner_of, block_row, block_col, me_index, capacity):
-    owned = (owner_of[:, 0] == me_index).astype(jnp.int32)
-    ranks = jnp.cumsum(owned) - 1
-    slots = jnp.arange(capacity, dtype=jnp.int32)
-    match = (owned[None, :] == 1) & (ranks[None, :] == slots[:, None])
-    live = jnp.any(match, axis=1).astype(jnp.float32)
-    slot_rows = jnp.sum(jnp.where(match, block_row[None, :], 0), axis=1)
-    slot_cols = jnp.sum(jnp.where(match, block_col[None, :], 0), axis=1)
-    return (slot_rows, slot_cols, live)
+def sorted_places(owner_of, block_row, block_col, plane):
+    owners = jnp.arange(N_OWNER, dtype=jnp.int32)
+    named = (owner_of[:, 0][None, :] == owners[:, None]).astype(jnp.int32)
+    running = jnp.cumsum(named, axis=1)
+    counts = running[:, -1]
+    starts = jnp.sum(jnp.where(owners[None, :] < owners[:, None], counts[None, :], 0), axis=1)
+    spot = jnp.sum(named * (running - 1 + starts[:, None]), axis=0)
+    place = jnp.arange(CHUNKS * 4 * CHIPS, dtype=jnp.int32)
+    chunk, pos, chip = place // (4 * CHIPS), (place // CHIPS) % 4, place % CHIPS
+    wanted = CHIPS * (24 * pos + CHUNKS * plane + chunk) + chip
+    packed = block_row * 32 + block_col
+    listed = jnp.sum(jnp.where(wanted[:, None] == spot[None, :], packed[None, :], 0), axis=1)
+    return listed, starts, counts
 
 
 def wrap(value, size):
     return lax.rem(value, size)
 
 
-def kernel(items, row_ref, col_ref, live_ref, hidden_hbm, grad_hbm, slot_grad_ref, total_ref,
+def kernel(items, share, place_ref, start_ref, count_ref, hidden_hbm, grad_hbm, slot_grad_ref, total_ref,
            hidden, grad, grad_t, to_pair, from_pair, chip, ring_a, ring_b, line, last_a, last_b,
-           sums, sum_in, load_sem, send_sem, recv_sem, sum_send, sum_recv):
+           done_0, done_1, done_2, to_owner, gathered, to_slot, landed,
+           sums, sum_in, load_sem, send_sem, recv_sem, move_send, move_recv, sum_send, sum_recv):
     f32, bf16 = jnp.float32, jnp.bfloat16
     d = lax.axis_index("dp")
     z = lax.axis_index("owner")
@@ -63,7 +69,9 @@
     groups = [[partner], [near(0, k) for k in (1, 2, 3)], [near(1, k) for k in (1, 2, 3)],
               [up(k) for k in range(1, N_OWNER)]]
     barrier = pltpu.get_barrier_semaphore()
-    everyone = [who for group in groups for who in group]
+    offsets = [(dx, dy) for dx in range(4) for dy in range(4) if dx or dy]
+    spread = [device(wrap(x + dx, 4), wrap(y + dy, 4), c) for dx, dy in offsets]
+    everyone = [partner] + spread + groups[3]
     for who in everyone:
         pl.semaphore_signal(barrier, inc=1, device_id=who, device_id_type=MESH)
 
@@ -75,7 +83,6 @@
 
     lax.fori_loop(0, grad_t.shape[0], turn, 0)
     pltpu.make_async_copy(hidden, hidden, load_sem.at[1]).wait()
-    pl.semaphore_wait(barrier, len(everyone))
 
     started = []
 
@@ -92,8 +99,9 @@
     def arrive(item, kind):
         arrivals[item, kind].wait_recv()
 
-    def product(slot):
-        row, col = row_ref[slot], col_ref[slot]
+    def product(place):
+        both_indices = place_ref[place]
+        row, col = lax.shift_right_logical(both_indices, 5), both_indices & 31
         return jnp.dot(grad_t[col], hidden[row], preferred_element_type=f32)
 
     def slot_of(item, ra, rb, core):
@@ -101,7 +109,7 @@
             px, py = wrap(x + ra, 4), wrap(y + rb, 4)
         else:
             px, py = wrap(x + rb, 4), wrap(y + ra, 4)
-        return ((px * 4 + py) * 2 + core) * items + item
+        return ((item // 2) * 4 + 2 * core + item % 2) * CHIPS + px * 4 + py
 
     def partner_products(item):
         def body(ra, carry):
@@ -109,6 +117,8 @@
                 to_pair[item, ra * 4 + rb] = product(slot_of(item, ra, rb, 1 - c)).astype(bf16)
             return carry
         lax.fori_loop(0, 4, body, 0)
+        if item == 0:
+            pl.semaphore_wait(barrier, len(everyone))
         send(to_pair.at[item], from_pair.at[item], item, PAIR, partner)
 
     def own_products(item):
@@ -166,55 +176,165 @@
         for kind in (YB0, YB0 + 1, YB1, YB1 + 1):
             arrive(item, kind)
         value = (line[item, 0].astype(f32) + last_b[item, 0].astype(f32) + last_b[item, 1].astype(f32))
-        value = value * live_ref[d * items + item]
-        slot_grad_ref[item] = value.T
+        done[item // 2][c * 2 + item % 2] = value.astype(bf16)
         return jnp.sum((value * value).reshape(-1, 8, BLOCK), axis=0)
 
-    steps = items // 2
-    part = jnp.zeros((8, BLOCK), f32)
-    both = lambda stage, step: [stage(2 * step + q) for q in (0, 1)] if 0 <= step < steps else []
-    for tick in range(-1, steps + 4):
-        both(partner_products, tick + 1)
-        both(own_products, tick)
-        both(ring_step, tick - 1)
-        both(line_step, tick - 3)
-        both(ring_end, tick - 2)
-        for piece in both(finish, tick - 4):
-            part = part + piece
-
-    sums[0] = part
-    first = 0
-    for n, group in enumerate(groups):
-        for k, who in enumerate(group):
+    done = (done_0, done_1, done_2)
+    me_chip = x * 4 + y
+    half = BLOCK // 2
+    mine = pl.ds(pl.multiple_of(c * half, half), half)
+    moves = {}
+
+    def move(src, dst, index, who):
+        copy = pltpu.make_async_remote_copy(
+            src_ref=src, dst_ref=dst, send_sem=move_send.at[index], recv_sem=move_recv.at[index],
+            device_id=who, device_id_type=MESH)
+        copy.start()
+        started.append(copy)
+        moves[index] = copy
+
+    def share_done(chunk):
+        move(done[chunk].at[pl.ds(2 * c, 2)], done[chunk].at[pl.ds(2 * c, 2)], chunk, partner)
+
+    def held_for(chunk, owner):
+        first = start_ref[owner] - me_chip - CHIPS * (CHUNKS * z + chunk) + 383
+        pos = jnp.minimum(lax.div(jnp.maximum(first, 0), 384), 3)
+        return done[chunk][pos]
+
+    def to_owners(chunk):
+        moves[chunk].wait_recv()
+        base = 3 + 6 * chunk
+        for j in (1, 2, 0):
+            owner = wrap(z + 2 * j + 1 + c, N_OWNER)
+            to_owner[chunk, j] = held_for(chunk, owner)
+            move(to_owner.at[chunk, j], gathered.at[chunk * 8 + c * 3 + j], base + j, {"owner": owner})
+        owner = wrap(z + 7, N_OWNER)
+        to_owner[chunk, 3] = held_for(chunk, owner)
+        move(to_owner.at[chunk, 3, mine], gathered.at[chunk * 8 + 6, mine], base + 3, {"owner": owner})
+        gathered[chunk * 8 + 7] = held_for(chunk, z)
+
+    def share_gathered(chunk):
+        base = 3 + 6 * chunk
+        for j in range(4):
+            moves[base + j].wait_recv()
+        trio = gathered.at[pl.ds(chunk * 8 + c * 3, 3)]
+        move(trio, trio, base + 4, partner)
+        rest = gathered.at[chunk * 8 + 6, mine]
+        move(rest, rest, base + 5, partner)
+
+    start, count = start_ref[z], count_ref[z]
+
+    def block_for(to_chip):
+        first = start + share * (2 * to_chip + c)
+        spot = first + ((me_chip - first) & (CHIPS - 1))
+        q = jnp.minimum(lax.div(spot, CHIPS), 95)
+        chunk = wrap(q, CHUNKS)
+        away = (z - lax.div(q, CHUNKS)) & (N_OWNER - 1)
+        index = 3 * ((away + 1) & 1) + lax.shift_right_logical(away + 7, 1) - 4
+        index = jnp.where(away == 0, 7, jnp.where(away == 7, 6, index))
+        return gathered[chunk * 8 + index]
+
+    def to_slots():
+        for chunk in range(CHUNKS):
+            moves[3 + 6 * chunk + 4].wait_recv()
+            moves[3 + 6 * chunk + 5].wait_recv()
+        base = 3 + 6 * CHUNKS
+        for k, (dx, dy) in enumerate(offsets):
+            to_slot[k] = block_for(wrap(x + dx, 4) * 4 + wrap(y + dy, 4))
+            move(to_slot.at[k], landed.at[me_chip], base + k, spread[k])
+        landed[me_chip] = block_for(me_chip)
+
+    def store_slots():
+        for k in range(len(offsets)):
+            moves[3 + 6 * CHUNKS + k].wait_recv()
+        for i in range(share):
+            slot = d * share + i
+            value = landed[(start + slot) & (CHIPS - 1)].astype(f32)
+            slot_grad_ref[i] = (value * (slot < count).astype(f32)).T
+
+    def add_start(n, value):
+        first = sum(len(group) for group in groups[:n])
+        sums[n] = value
+        copies = []
+        for k, who in enumerate(groups[n]):
             copy = pltpu.make_async_remote_copy(
                 src_ref=sums.at[n], dst_ref=sum_in.at[first + k], send_sem=sum_send.at[first + k],
                 recv_sem=sum_recv.at[first + k], device_id=who, device_id_type=MESH)
             copy.start()
             started.append(copy)
-        for k, copy in enumerate(started[-len(group):]):
+            copies.append((first + k, copy))
+        return copies
+
+    def add_end(value, copies):
+        for k, copy in copies:
             copy.wait_recv()
-            part = part + sum_in[first + k]
-        first += len(group)
-        if n + 1 < len(groups):
-            sums[n + 1] = part
-    total_ref[...] = part
+            value = value + sum_in[k]
+        return value
+
+    part = jnp.zeros((8, BLOCK), f32)
+
+    def pair(stage, chunk):
+        return [stage(2 * chunk), stage(2 * chunk + 1)]
+
+    def close(chunk, value):
+        for piece in pair(finish, chunk):
+            value = value + piece
+        share_done(chunk)
+        return value
+
+    pair(partner_products, 0)
+    pair(partner_products, 1)
+    pair(own_products, 0)
+    pair(partner_products, 2)
+    pair(own_products, 1)
+    pair(ring_step, 0)
+    pair(own_products, 2)
+    pair(ring_step, 1)
+    pair(ring_end, 0)
+    pair(ring_step, 2)
+    pair(line_step, 0)
+    pair(ring_end, 1)
+    part = close(0, part)
+    pair(ring_end, 2)
+    pair(line_step, 1)
+    to_owners(0)
+    part = close(1, part)
+    pair(line_step, 2)
+    share_gathered(0)
+    to_owners(1)
+    part = close(2, part)
+    copies = add_start(0, part)
+    share_gathered(1)
+    to_owners(2)
+    part = add_end(part, copies)
+    copies = add_start(1, part)
+    share_gathered(2)
+    part = add_end(part, copies)
+    copies = add_start(2, part)
+    to_slots()
+    part = add_end(part, copies)
+    copies = add_start(3, part)
+    store_slots()
+    part = add_end(part, copies)
+    total_ref[0, 0] = jnp.sum(part)
     for copy in started:
         copy.wait_send()
 
 
-def reduce_blocks(rows, cols, live, hidden, grad_out, items):
+def reduce_blocks(places, starts, counts, hidden, grad_out, share):
     tokens, features = hidden.shape[0], grad_out.shape[1]
     bf16, f32 = jnp.bfloat16, jnp.float32
+    items = 2 * CHUNKS
     peers = 1 + 3 + 3 + N_OWNER - 1
     block = (BLOCK, BLOCK)
     smem = pl.BlockSpec(memory_space=pltpu.SMEM)
     vmem = pl.BlockSpec(memory_space=pltpu.VMEM)
     hbm = pl.BlockSpec(memory_space=pl.ANY)
     return pl.pallas_call(
-        functools.partial(kernel, items),
-        out_shape=(jax.ShapeDtypeStruct((items, *block), f32), jax.ShapeDtypeStruct((8, BLOCK), f32)),
+        functools.partial(kernel, items, share),
+        out_shape=(jax.ShapeDtypeStruct((share, *block), f32), jax.ShapeDtypeStruct((1, 1), f32)),
         in_specs=[smem, smem, smem, hbm, hbm],
-        out_specs=(vmem, vmem),
+        out_specs=(vmem, smem),
         scratch_shapes=[
             pltpu.VMEM((hidden.shape[1] // BLOCK, tokens, BLOCK), bf16),
             pltpu.VMEM((features // BLOCK, tokens, BLOCK), bf16),
@@ -227,27 +347,34 @@
             pltpu.VMEM((items, 4, *block), bf16),
             pltpu.VMEM((items, 2, BLOCK // 2, BLOCK), bf16),
             pltpu.VMEM((items, 2, *block), bf16),
+            pltpu.VMEM((4, *block), bf16),
+            pltpu.VMEM((4, *block), bf16),
+            pltpu.VMEM((4, *block), bf16),
+            pltpu.VMEM((CHUNKS, 4, *block), bf16),
+            pltpu.VMEM((CHUNKS * N_OWNER, *block), bf16),
+            pltpu.VMEM((CHIPS - 1, *block), bf16),
+            pltpu.VMEM((CHIPS, *block), bf16),
             pltpu.VMEM((4, 8, BLOCK), f32),
             pltpu.VMEM((peers, 8, BLOCK), f32),
             pltpu.SemaphoreType.DMA((2,)),
             pltpu.SemaphoreType.DMA((items, 13)),
             pltpu.SemaphoreType.DMA((items, 13)),
+            pltpu.SemaphoreType.DMA((7 * CHUNKS + CHIPS - 1,)),
+            pltpu.SemaphoreType.DMA((7 * CHUNKS + CHIPS - 1,)),
             pltpu.SemaphoreType.DMA((peers,)),
             pltpu.SemaphoreType.DMA((peers,)),
         ],
         compiler_params=pltpu.CompilerParams(
             collective_id=0, has_side_effects=True, vmem_limit_bytes=62 * 1024 * 1024),
         name="reduce_blocks",
-    )(rows, cols, live, hidden, grad_out)
+    )(places, starts, counts, hidden, grad_out)
 
 
 def on_device(hidden, grad_out, block_row, block_col, owner_of, master, moment1, moment2):
     share = master.shape[1]
-    me_index = lax.axis_index("owner")
-    rows, cols, live = slot_table(owner_of, block_row, block_col, me_index, CAP)
-    shares, parts = reduce_blocks(rows, cols, live, hidden, grad_out, share)
-    total = jnp.sum(parts)
-    clip = 1.0 / jnp.maximum(jnp.sqrt(total), 1.0)
+    places, starts, counts = sorted_places(owner_of, block_row, block_col, lax.axis_index("owner"))
+    shares, total = reduce_blocks(places, starts, counts, hidden, grad_out, share)
+    clip = 1.0 / jnp.maximum(jnp.sqrt(total[0, 0]), 1.0)
     scaled = clip * shares[None]
     first = 0.9 * moment1 + 0.1 * scaled
     second = 0.95 * moment2 + 0.05 * scaled * scaled

time: 85.3 us -> 76.6 us (0.90)
  Pallas kernels: 74.8 us -> 67.2 us
  other arithmetic: 9.15 us -> 7.89 us
    pallas_call x1, Pallas kernels: 74.8 us -> 67.2 us  [reduce_blocks(): pl.pallas_call(functools.partial(kernel, items, share), out_shape=(jax.Sh...]
    reduce_sum x2 -> x3, other arithmetic: 3.49 us -> 1.04 us  [the longest x1 0.83 us: sorted_places(): jnp.sum(jnp.where(wanted[:, None] == spot[None, :], packed[None, :], 0),...]
    another operation x2, other arithmetic: 0.32 us -> 2.45 us
    convert_element_type x2 -> x1, other arithmetic: 1.28 us -> 0.01 us  [sorted_places(): named = (owner_of[:, 0][None, :] == owners[:, None]).astype(jnp.int32)]
where the time goes in v2:
time: 76.6 us; the launch traced here: 76.4 us
  Pallas kernels  67.2 us (88%)
  other arithmetic  7.89 us (10%)
  between operations  0.79 us (1%)
    pallas_call x1, Pallas kernels, reduce_blocks(): pl.pallas_call(functools.partial(kernel, items, share), out_shape=(jax.Sh...  67.2 us
    sub x1, other arithmetic, on_device(): return master - 0.25 * (direction + 0.1 * master)  2.87 us
    another operation x2, other arithmetic  2.45 us

profile of v2, /device:TPU:1, one launch (start us, length us, event | category | flops | bytes accessed | tf_op | source)
XLA Modules:
  0.0 76.4 jit_solution(18258371167476404482)
XLA Ops:
  0.0 0.7 multiply_add_fusion
  0.7 0.7 reduce.1
  1.5 2.3 %reduce-window.6 = s32[8,12,128]{2,1,0:T(8,128)S(1)} reduce-window(s32[8,12,128]{2,1,0:T(8,128)S(1)} %fusion.8, s32[]{:T(128)} %constant.76.clone.1), window={size=1x1x128 pad=0_0x0_0x127_0}, to_apply=%region_0.0 | reduce-window | flops 1560576 | bytes 98308 | tf_op jit(solution)/shard_map/reduce-window
  3.7 0.3 slice_reduce_fusion
  4.0 0.2 reduce-window.9
  4.2 0.1 add_bitcast_fusion
  4.3 0.2 slice_reduce_fusion.1.count_ref
  4.5 0.0 copy-start.3
  4.5 0.1 select_reduce_fusion.2.start_ref
  4.6 0.0 copy-start.2
  4.6 0.1 select_reduce_fusion.1
  4.7 0.8 %select_reduce_fusion.place_ref = s32[192]{0:T(256)} fusion(s32[1536]{0:T(1024)S(1)} %multiply_add_fusion, s32[1536]{0:T(1024)S(1)} %bitcast.38, s32[192]{0:T(256)S(1)} %fusion.11), kind=kLoop, calls=%fused_computation.1 | loop fusion | flops 884544 | bytes 13824 | tf_op jit(solution)/shard_map/reduce_sum | solution.py:29
  5.6 0.0 copy-done.3
  5.6 0.0 copy-done.2
  5.6 0.0 copy-start
  5.6 0.0 copy-start.1
  5.6 67.2 %reduce_blocks.1 = (f32[12,128,128]{2,1,0:T(8,128)}, f32[1,1]{1,0:T(1,128)}) custom-call(s32[192]{0:T(256)} %select_reduce_fusion.place_ref, s32[8]{0:T(128)} %copy-done.2, s32[8]{0:T(128)} %copy-done.3, bf16[256,14336]{1,0:T(8,128)(2,1)} %hidden_hbm.1, bf16[256,4096]{1,0:T(8,128)(2,1)} %grad_hbm.1), custom_call_target="tpu_custom_call" | custom-call | tf_op jit(solution)/shard_map/reduce_blocks/pallas_call | solution.py:333
  73.5 0.0 copy-done
  73.5 0.0 copy-done.1
  73.5 2.9 %multiply_subtract_fusion = f32[1,12,128,128]{3,2,1,0:T(8,128)} fusion(f32[1,12,128,128]{3,2,1,0:T(8,128)S(1)} %copy-done, f32[1,12,128,128]{3,2,1,0:T(8,128)S(1)} %copy-done.1, f32[12,128,128]{2,1,0:T(8,128)} %get-tuple-element.8, f32[1,12,128,128]{3,2,1,0:T(8,128)} %param.14, f32[]{:T(128)} %bitcast.1), kind=kLoop, calls=%fused_computation.11 | loop fusion | flops 3145728 | bytes 3932164 | tf_op jit(solution)/shard_map/sub | solution.py:382
  (3 shorter events, 0.0 us)
Async XLA Ops:
  4.5 1.1 %copy-start.3 = (s32[8]{0:T(128)}, s32[8]{0:T(128)S(1)}, u32[]{:S(2)}) copy-start(s32[8]{0:T(128)S(1)} %slice_reduce_fusion.1.count_ref) | copy-start | bytes 100
  4.6 0.9 %copy-start.2 = (s32[8]{0:T(128)}, s32[8]{0:T(128)S(1)}, u32[]{:S(2)}) copy-start(s32[8]{0:T(128)S(1)} %select_reduce_fusion.2.start_ref) | copy-start | bytes 100
  5.6 67.9 %copy-start = (f32[1,12,128,128]{3,2,1,0:T(8,128)S(1)}, f32[1,12,128,128]{3,2,1,0:T(8,128)}, u32[]{:S(2)}) copy-start(f32[1,12,128,128]{3,2,1,0:T(8,128)} %param.13) | copy-start | bytes 2359300
  5.6 67.9 %copy-start.1 = (f32[1,12,128,128]{3,2,1,0:T(8,128)S(1)}, f32[1,12,128,128]{3,2,1,0:T(8,128)}, u32[]{:S(2)}) copy-start(f32[1,12,128,128]{3,2,1,0:T(8,128)} %param.15) | copy-start | bytes 2359300

commit v3 on v2

--- a/solution.py
+++ b/solution.py
@@ -56,16 +56,6 @@
     def up(step):
         return {"owner": wrap(z + step, N_OWNER)}
 
-    def load(src, dst, sem):
-        def body(k, carry):
-            columns = pl.ds(pl.multiple_of(k * BLOCK, BLOCK), BLOCK)
-            pltpu.make_async_copy(src.at[:, columns], dst.at[k], sem).start()
-            return carry
-        lax.fori_loop(0, dst.shape[0], body, 0)
-
-    load(grad_hbm, grad, load_sem.at[0])
-    load(hidden_hbm, hidden, load_sem.at[1])
-
     groups = [[partner], [near(0, k) for k in (1, 2, 3)], [near(1, k) for k in (1, 2, 3)],
               [up(k) for k in range(1, N_OWNER)]]
     barrier = pltpu.get_barrier_semaphore()
@@ -75,13 +65,38 @@
     for who in everyone:
         pl.semaphore_signal(barrier, inc=1, device_id=who, device_id_type=MESH)
 
+    def load(src, dst, sem, k):
+        columns = pl.ds(pl.multiple_of(k * BLOCK, BLOCK), BLOCK)
+        pltpu.make_async_copy(src.at[:, columns], dst.at[k], sem).start()
+
+    def load_grad(k, carry):
+        load(grad_hbm, grad, load_sem.at[0], k)
+        return carry
+
+    lax.fori_loop(0, grad.shape[0], load_grad, 0, unroll=8)
+
+    def load_hidden(k, carry):
+        load(hidden_hbm, hidden, load_sem.at[1], k)
+        return carry
+
+    early = hidden.shape[0] // 2
+    lax.fori_loop(0, early, load_hidden, 0, unroll=8)
     pltpu.make_async_copy(grad, grad, load_sem.at[0]).wait()
 
     def turn(k, carry):
+        for n in range(2):
+            load(hidden_hbm, hidden, load_sem.at[1], early + 2 * k + n)
         grad_t[k] = grad[k].T
         return carry
 
-    lax.fori_loop(0, grad_t.shape[0], turn, 0)
+    late = hidden.shape[0] - early
+    lax.fori_loop(0, late // 2, turn, 0, unroll=4)
+
+    def turn_only(k, carry):
+        grad_t[k] = grad[k].T
+        return carry
+
+    lax.fori_loop(late // 2, grad.shape[0], turn_only, 0, unroll=4)
     pltpu.make_async_copy(hidden, hidden, load_sem.at[1]).wait()
 
     started = []
@@ -112,11 +127,8 @@
         return ((item // 2) * 4 + 2 * core + item % 2) * CHIPS + px * 4 + py
 
     def partner_products(item):
-        def body(ra, carry):
-            for rb in range(4):
-                to_pair[item, ra * 4 + rb] = product(slot_of(item, ra, rb, 1 - c)).astype(bf16)
-            return carry
-        lax.fori_loop(0, 4, body, 0)
+        for j in range(CHIPS):
+            to_pair[item, j] = product(slot_of(item, j // 4, j % 4, 1 - c)).astype(bf16)
         if item == 0:
             pl.semaphore_wait(barrier, len(everyone))
         send(to_pair.at[item], from_pair.at[item], item, PAIR, partner)
@@ -124,13 +136,9 @@
     def own_products(item):
         arrive(item, PAIR)
 
-        def body(ra, carry):
-            for rb in range(4):
-                j = ra * 4 + rb
-                value = product(slot_of(item, ra, rb, c)) + from_pair[item, j].astype(f32)
-                chip[item, j] = value.astype(bf16)
-            return carry
-        lax.fori_loop(0, 4, body, 0)
+        for j in range(CHIPS):
+            value = product(slot_of(item, j // 4, j % 4, c)) + from_pair[item, j].astype(f32)
+            chip[item, j] = value.astype(bf16)
         axis = item % 2
         send(chip.at[item, pl.ds(8, 2)], ring_a.at[item, 0], item, XA, near(axis, 1))
         send(chip.at[item, pl.ds(10, 2)], ring_a.at[item, 1], item, XA + 1, near(axis, 3))
@@ -300,14 +308,14 @@
     to_owners(0)
     part = close(1, part)
     pair(line_step, 2)
-    share_gathered(0)
     to_owners(1)
     part = close(2, part)
     copies = add_start(0, part)
-    share_gathered(1)
     to_owners(2)
+    share_gathered(0)
     part = add_end(part, copies)
     copies = add_start(1, part)
+    share_gathered(1)
     share_gathered(2)
     part = add_end(part, copies)
     copies = add_start(2, part)

time: 76.6 us -> 69 us (0.901)
  Pallas kernels: 67.2 us -> 59.6 us
    pallas_call x1, Pallas kernels: 67.2 us -> 59.6 us  [reduce_blocks(): pl.pallas_call(functools.partial(kernel, items, share), out_shape=(jax.Sh...]
where the time goes in v3:
time: 69 us; the launch traced here: 68.8 us
  Pallas kernels  59.6 us (86%)
  other arithmetic  7.89 us (11%)
  between operations  0.79 us (1%)
    pallas_call x1, Pallas kernels, reduce_blocks(): pl.pallas_call(functools.partial(kernel, items, share), out_shape=(jax.Sh...  59.6 us
    sub x1, other arithmetic, on_device(): return master - 0.25 * (direction + 0.1 * master)  2.87 us
    another operation x2, other arithmetic  2.45 us

profile of v3, /device:TPU:1, one launch (start us, length us, event | category | flops | bytes accessed | tf_op | source)
XLA Modules:
  0.0 68.8 jit_solution(1135135516675115999)
XLA Ops:
  0.0 0.7 %multiply_add_fusion = s32[1536]{0:T(1024)S(1)} fusion(s32[1536]{0:T(1024)} %param.11, s32[1536]{0:T(1024)} %param.10), kind=kLoop, calls=%fused_computation.18 | loop fusion | flops 3072 | bytes 18432 | tf_op jit(solution)/shard_map/add | solution.py:28
  0.7 0.7 %reduce.1 = s32[1536]{0:T(1024)S(1)} reduce(s32[1536,1]{0,1:T(1,128)} %param.12, s32[]{:T(128)} %constant.76.clone.1), dimensions={1}, to_apply=%param.12.reduce_sub_computation | reduce | bytes 12292 | tf_op args[4]
  1.5 2.3 %reduce-window.6 = s32[8,12,128]{2,1,0:T(8,128)S(1)} reduce-window(s32[8,12,128]{2,1,0:T(8,128)S(1)} %fusion.8, s32[]{:T(128)} %constant.76.clone.1), window={size=1x1x128 pad=0_0x0_0x127_0}, to_apply=%region_0.0 | reduce-window | flops 1560576 | bytes 98308 | tf_op jit(solution)/shard_map/reduce-window
  3.7 0.3 slice_reduce_fusion
  4.0 0.2 reduce-window.9
  4.2 0.1 add_bitcast_fusion
  4.3 0.2 slice_reduce_fusion.1.count_ref
  4.5 0.0 copy-start.3
  4.5 0.1 select_reduce_fusion.2.start_ref
  4.6 0.0 copy-start.2
  4.6 0.1 select_reduce_fusion.1
  4.7 0.8 %select_reduce_fusion.place_ref = s32[192]{0:T(256)} fusion(s32[1536]{0:T(1024)S(1)} %multiply_add_fusion, s32[1536]{0:T(1024)S(1)} %bitcast.38, s32[192]{0:T(256)S(1)} %fusion.11), kind=kLoop, calls=%fused_computation.1 | loop fusion | flops 884544 | bytes 13824 | tf_op jit(solution)/shard_map/reduce_sum | solution.py:29
  5.6 0.0 copy-done.3
  5.6 0.0 copy-done.2
  5.6 0.0 copy-start
  5.6 0.0 copy-start.1
  5.6 59.6 %reduce_blocks.1 = (f32[12,128,128]{2,1,0:T(8,128)}, f32[1,1]{1,0:T(1,128)}) custom-call(s32[192]{0:T(256)} %select_reduce_fusion.place_ref, s32[8]{0:T(128)} %copy-done.2, s32[8]{0:T(128)} %copy-done.3, bf16[256,14336]{1,0:T(8,128)(2,1)} %hidden_hbm.1, bf16[256,4096]{1,0:T(8,128)(2,1)} %grad_hbm.1), custom_call_target="tpu_custom_call" | custom-call | tf_op jit(solution)/shard_map/reduce_blocks/pallas_call | solution.py:341
  65.9 0.0 copy-done
  65.9 0.0 copy-done.1
  65.9 2.9 %multiply_subtract_fusion = f32[1,12,128,128]{3,2,1,0:T(8,128)} fusion(f32[1,12,128,128]{3,2,1,0:T(8,128)S(1)} %copy-done, f32[1,12,128,128]{3,2,1,0:T(8,128)S(1)} %copy-done.1, f32[12,128,128]{2,1,0:T(8,128)} %get-tuple-element.8, f32[1,12,128,128]{3,2,1,0:T(8,128)} %param.14, f32[]{:T(128)} %bitcast.1), kind=kLoop, calls=%fused_computation.11 | loop fusion | flops 3145728 | bytes 3932164 | tf_op jit(solution)/shard_map/sub | solution.py:390
  (3 shorter events, 0.0 us)
Async XLA Ops:
  4.5 1.1 %copy-start.3 = (s32[8]{0:T(128)}, s32[8]{0:T(128)S(1)}, u32[]{:S(2)}) copy-start(s32[8]{0:T(128)S(1)} %slice_reduce_fusion.1.count_ref) | copy-start | bytes 100
  4.6 0.9 %copy-start.2 = (s32[8]{0:T(128)}, s32[8]{0:T(128)S(1)}, u32[]{:S(2)}) copy-start(s32[8]{0:T(128)S(1)} %select_reduce_fusion.2.start_ref) | copy-start | bytes 100
  5.6 60.3 %copy-start = (f32[1,12,128,128]{3,2,1,0:T(8,128)S(1)}, f32[1,12,128,128]{3,2,1,0:T(8,128)}, u32[]{:S(2)}) copy-start(f32[1,12,128,128]{3,2,1,0:T(8,128)} %param.13) | copy-start | bytes 2359300
  5.6 60.3 %copy-start.1 = (f32[1,12,128,128]{3,2,1,0:T(8,128)S(1)}, f32[1,12,128,128]{3,2,1,0:T(8,128)}, u32[]{:S(2)}) copy-start(f32[1,12,128,128]{3,2,1,0:T(8,128)} %param.15) | copy-start | bytes 2359300

commit v4 on v3

--- a/solution.py
+++ b/solution.py
@@ -15,27 +15,12 @@
 PAIR, XA, XB0, XB1, YA, YB0, YB1 = 0, 1, 3, 5, 7, 9, 11
 
 
-def sorted_places(owner_of, block_row, block_col, plane):
-    owners = jnp.arange(N_OWNER, dtype=jnp.int32)
-    named = (owner_of[:, 0][None, :] == owners[:, None]).astype(jnp.int32)
-    running = jnp.cumsum(named, axis=1)
-    counts = running[:, -1]
-    starts = jnp.sum(jnp.where(owners[None, :] < owners[:, None], counts[None, :], 0), axis=1)
-    spot = jnp.sum(named * (running - 1 + starts[:, None]), axis=0)
-    place = jnp.arange(CHUNKS * 4 * CHIPS, dtype=jnp.int32)
-    chunk, pos, chip = place // (4 * CHIPS), (place // CHIPS) % 4, place % CHIPS
-    wanted = CHIPS * (24 * pos + CHUNKS * plane + chunk) + chip
-    packed = block_row * 32 + block_col
-    listed = jnp.sum(jnp.where(wanted[:, None] == spot[None, :], packed[None, :], 0), axis=1)
-    return listed, starts, counts
-
-
 def wrap(value, size):
     return lax.rem(value, size)
 
 
-def kernel(items, share, place_ref, start_ref, count_ref, hidden_hbm, grad_hbm, slot_grad_ref, total_ref,
-           hidden, grad, grad_t, to_pair, from_pair, chip, ring_a, ring_b, line, last_a, last_b,
+def kernel(items, share, listed, row_ref, col_ref, owner_ref, hidden_hbm, grad_hbm, slot_grad_ref, total_ref,
+           spots_v, starts_v, spots, starts, hidden, grad, grad_t, to_pair, from_pair, chip, ring_a, ring_b, line, last_a, last_b,
            done_0, done_1, done_2, to_owner, gathered, to_slot, landed,
            sums, sum_in, load_sem, send_sem, recv_sem, move_send, move_recv, sum_send, sum_recv):
     f32, bf16 = jnp.float32, jnp.bfloat16
@@ -79,8 +64,41 @@
         load(hidden_hbm, hidden, load_sem.at[1], k)
         return carry
 
+    def make_places():
+        square = (BLOCK, BLOCK)
+        lines = listed // BLOCK
+        up_to = lax.broadcasted_iota(jnp.int32, square, 0) <= lax.broadcasted_iota(jnp.int32, square, 1)
+        below = lax.broadcasted_iota(jnp.int32, square, 1) < lax.broadcasted_iota(jnp.int32, square, 0)
+        owners = owner_ref[...]
+        named = jnp.concatenate([(owners == o).astype(f32) for o in range(N_OWNER)], axis=0)
+        named_16 = named.astype(bf16)
+        along = jnp.dot(named_16, up_to.astype(f32).astype(bf16), preferred_element_type=f32)
+        line_sums = jnp.dot(named_16, jnp.ones(square, bf16), preferred_element_type=f32)
+        before = jnp.dot(below.astype(f32).astype(bf16), line_sums.astype(bf16), preferred_element_type=f32)
+        spot = jnp.sum((named * (before + along - 1.0)).reshape(N_OWNER, -1, BLOCK), axis=0)
+        starts_v[...] = before.reshape(N_OWNER, -1, BLOCK)[:, 0].astype(jnp.int32)
+        spot_t = jnp.pad(spot, ((0, BLOCK - spot.shape[0]), (0, 0))).T
+        wide = (BLOCK, 2 * BLOCK)
+        place = lax.broadcasted_iota(jnp.int32, wide, 1)
+        chip_of, pos, chunk = place & (CHIPS - 1), lax.shift_right_logical(place, 4) & 3, lax.shift_right_logical(place, 6)
+        wanted = (CHIPS * (24 * pos + CHUNKS * z + chunk) + chip_of).astype(f32)
+        which = lax.broadcasted_iota(jnp.int32, (8, BLOCK), 0)
+        found = jnp.zeros((8, 2 * BLOCK), f32)
+        for r in range(lines):
+            hit = jnp.where(spot_t[:, r:r + 1] == wanted, 1.0, 0.0).astype(bf16)
+            value = jnp.where(which == 0, row_ref[r:r + 1, :], col_ref[r:r + 1, :]).astype(f32).astype(bf16)
+            found = found + jnp.dot(value, hit, preferred_element_type=f32)
+        spots_v[...] = found.astype(jnp.int32)
+        copies = [pltpu.make_async_copy(spots_v, spots, load_sem.at[2]),
+                  pltpu.make_async_copy(starts_v, starts, load_sem.at[3])]
+        for copy in copies:
+            copy.start()
+        for copy in copies:
+            copy.wait()
+
     early = hidden.shape[0] // 2
     lax.fori_loop(0, early, load_hidden, 0, unroll=8)
+    make_places()
     pltpu.make_async_copy(grad, grad, load_sem.at[0]).wait()
 
     def turn(k, carry):
@@ -115,8 +133,8 @@
         arrivals[item, kind].wait_recv()
 
     def product(place):
-        both_indices = place_ref[place]
-        row, col = lax.shift_right_logical(both_indices, 5), both_indices & 31
+        row = jnp.clip(spots[0, place], 0, hidden.shape[0] - 1)
+        col = jnp.clip(spots[1, place], 0, grad_t.shape[0] - 1)
         return jnp.dot(grad_t[col], hidden[row], preferred_element_type=f32)
 
     def slot_of(item, ra, rb, core):
@@ -205,7 +223,7 @@
         move(done[chunk].at[pl.ds(2 * c, 2)], done[chunk].at[pl.ds(2 * c, 2)], chunk, partner)
 
     def held_for(chunk, owner):
-        first = start_ref[owner] - me_chip - CHIPS * (CHUNKS * z + chunk) + 383
+        first = jnp.clip(starts[owner, 0], 0, listed) - me_chip - CHIPS * (CHUNKS * z + chunk) + 383
         pos = jnp.minimum(lax.div(jnp.maximum(first, 0), 384), 3)
         return done[chunk][pos]
 
@@ -230,7 +248,8 @@
         rest = gathered.at[chunk * 8 + 6, mine]
         move(rest, rest, base + 5, partner)
 
-    start, count = start_ref[z], count_ref[z]
+    start = jnp.clip(starts[z, 0], 0, listed)
+    count = jnp.where(z == N_OWNER - 1, listed, starts[jnp.minimum(z + 1, N_OWNER - 1), 0]) - start
 
     def block_for(to_chip):
         first = start + share * (2 * to_chip + c)
@@ -329,21 +348,27 @@
         copy.wait_send()
 
 
-def reduce_blocks(places, starts, counts, hidden, grad_out, share):
+def reduce_blocks(block_row, block_col, owner_of, hidden, grad_out, share):
+    listed = block_row.shape[0]
     tokens, features = hidden.shape[0], grad_out.shape[1]
     bf16, f32 = jnp.bfloat16, jnp.float32
     items = 2 * CHUNKS
     peers = 1 + 3 + 3 + N_OWNER - 1
     block = (BLOCK, BLOCK)
+    owners = jnp.pad(owner_of.reshape(-1, BLOCK), ((0, 16 - listed // BLOCK), (0, 0)), constant_values=-1)
     smem = pl.BlockSpec(memory_space=pltpu.SMEM)
     vmem = pl.BlockSpec(memory_space=pltpu.VMEM)
     hbm = pl.BlockSpec(memory_space=pl.ANY)
     return pl.pallas_call(
-        functools.partial(kernel, items, share),
+        functools.partial(kernel, items, share, listed),
         out_shape=(jax.ShapeDtypeStruct((share, *block), f32), jax.ShapeDtypeStruct((1, 1), f32)),
-        in_specs=[smem, smem, smem, hbm, hbm],
+        in_specs=[vmem, vmem, vmem, hbm, hbm],
         out_specs=(vmem, smem),
         scratch_shapes=[
+            pltpu.VMEM((8, 2 * BLOCK), jnp.int32),
+            pltpu.VMEM((N_OWNER, BLOCK), jnp.int32),
+            pltpu.SMEM((8, 2 * BLOCK), jnp.int32),
+            pltpu.SMEM((N_OWNER, BLOCK), jnp.int32),
             pltpu.VMEM((hidden.shape[1] // BLOCK, tokens, BLOCK), bf16),
             pltpu.VMEM((features // BLOCK, tokens, BLOCK), bf16),
             pltpu.VMEM((features // BLOCK, BLOCK, tokens), bf16),
@@ -364,7 +389,7 @@
             pltpu.VMEM((CHIPS, *block), bf16),
             pltpu.VMEM((4, 8, BLOCK), f32),
             pltpu.VMEM((peers, 8, BLOCK), f32),
-            pltpu.SemaphoreType.DMA((2,)),
+            pltpu.SemaphoreType.DMA((4,)),
             pltpu.SemaphoreType.DMA((items, 13)),
             pltpu.SemaphoreType.DMA((items, 13)),
             pltpu.SemaphoreType.DMA((7 * CHUNKS + CHIPS - 1,)),
@@ -375,13 +400,12 @@
         compiler_params=pltpu.CompilerParams(
             collective_id=0, has_side_effects=True, vmem_limit_bytes=62 * 1024 * 1024),
         name="reduce_blocks",
-    )(places, starts, counts, hidden, grad_out)
+    )(block_row.reshape(-1, BLOCK), block_col.reshape(-1, BLOCK), owners, hidden, grad_out)
 
 
 def on_device(hidden, grad_out, block_row, block_col, owner_of, master, moment1, moment2):
     share = master.shape[1]
-    places, starts, counts = sorted_places(owner_of, block_row, block_col, lax.axis_index("owner"))
-    shares, total = reduce_blocks(places, starts, counts, hidden, grad_out, share)
+    shares, total = reduce_blocks(block_row, block_col, owner_of, hidden, grad_out, share)
     clip = 1.0 / jnp.maximum(jnp.sqrt(total[0, 0]), 1.0)
     scaled = clip * shares[None]
     first = 0.9 * moment1 + 0.1 * scaled

time: 69 us -> 64 us (0.928)
  other arithmetic: 7.89 us -> 3.7 us
  Pallas kernels: 59.6 us -> 58.8 us
    another operation x2 -> x0, other arithmetic: 2.45 us -> none
    reduce_sum x3 -> x0, other arithmetic: 1.04 us -> none  [the longest x1 0.83 us: sorted_places(): jnp.sum(jnp.where(wanted[:, None] == spot[None, :], packed[None, :], 0),...]
    pallas_call x1, Pallas kernels: 59.6 us -> 58.8 us  [reduce_blocks(): pl.pallas_call(functools.partial(kernel, items, share, listed), out_shape...]
    add x2 -> x0, other arithmetic: 0.73 us -> none  [the longest x1 0.72 us: sorted_places(): packed = block_row * 32 + block_col]
where the time goes in v4:
time: 64 us; the launch traced here: 63.8 us
  Pallas kernels  58.8 us (92%)
  other arithmetic  3.7 us (6%)
  between operations  0.66 us (1%)
    pallas_call x1, Pallas kernels, reduce_blocks(): pl.pallas_call(functools.partial(kernel, items, share, listed), out_shape...  58.8 us
    sub x1, other arithmetic, on_device(): return master - 0.25 * (direction + 0.1 * master)  2.87 us

profile of v4, /device:TPU:1, one launch (start us, length us, event | category | flops | bytes accessed | tf_op | source)
XLA Modules:
  0.0 63.8 jit_solution(6766120598198176586)
XLA Ops:
  0.0 0.0 copy-start.1
  0.0 0.0 copy-start
  0.0 0.8 %reduce = s32[1536]{0:T(1024)S(1)} reduce(s32[1536,1]{0,1:T(1,128)} %param.12, s32[]{:T(128)} %constant.29), dimensions={1}, to_apply=%param.12.reduce_sub_computation | reduce | bytes 12292 | tf_op args[4]
  0.8 0.6 pad.4.owner_ref
  1.4 58.8 %reduce_blocks.1 = (f32[12,128,128]{2,1,0:T(8,128)}, f32[1,1]{1,0:T(1,128)}) custom-call(s32[12,128]{1,0:T(8,128)} %bitcast.29, s32[12,128]{1,0:T(8,128)} %bitcast.30, s32[16,128]{1,0:T(8,128)} %pad.4.owner_ref, bf16[256,14336]{1,0:T(8,128)(2,1)} %hidden_hbm.1, bf16[256,4096]{1,0:T(8,128)(2,1)} %grad_hbm.1), custom_call_target="tpu_custom_call" | custom-call | tf_op jit(solution)/shard_map/reduce_blocks/pallas_call | solution.py:362
  60.9 0.0 copy-done.1
  60.9 0.0 copy-done
  60.9 2.9 %multiply_subtract_fusion = f32[1,12,128,128]{3,2,1,0:T(8,128)} fusion(f32[1,12,128,128]{3,2,1,0:T(8,128)S(1)} %copy-done, f32[1,12,128,128]{3,2,1,0:T(8,128)S(1)} %copy-done.1, f32[12,128,128]{2,1,0:T(8,128)} %get-tuple-element.8, f32[1,12,128,128]{3,2,1,0:T(8,128)} %param.14, f32[]{:T(128)} %bitcast.2), kind=kLoop, calls=%fused_computation.10 | loop fusion | flops 3145728 | bytes 3932164 | tf_op jit(solution)/shard_map/sub | solution.py:414
Async XLA Ops:
  0.0 60.9 %copy-start.1 = (f32[1,12,128,128]{3,2,1,0:T(8,128)S(1)}, f32[1,12,128,128]{3,2,1,0:T(8,128)}, u32[]{:S(2)}) copy-start(f32[1,12,128,128]{3,2,1,0:T(8,128)} %param.15) | copy-start | bytes 2359300
  0.0 60.9 %copy-start = (f32[1,12,128,128]{3,2,1,0:T(8,128)S(1)}, f32[1,12,128,128]{3,2,1,0:T(8,128)}, u32[]{:S(2)}) copy-start(f32[1,12,128,128]{3,2,1,0:T(8,128)} %param.13) | copy-start | bytes 2359300

commit v5 on v4

v5 whole, which is shorter than its diff:
```python
import functools

import jax
import jax.numpy as jnp
from jax import lax
from jax.experimental import pallas as pl
from jax.experimental.pallas import tpu as pltpu
from jax.sharding import PartitionSpec as P

BLOCK = 128
N_OWNER = 8
MESH = pl.DeviceIdType.MESH
CHUNKS = 3
ORDER = (
    "P2P3P5P4O2A2O3A3B2P0B3O4A4O5A5P1R2R3B5O0A0B4R4R5O1E2E3A1B1R0",
    "E5E4L3B0L2R1L5L4F3F2s1E0E1F5F4s2z1L0L1z2F0F1s0a0z0a0g2g1a0g0",
)
CHIPS = 16
PAIR, XA, XB, YA, YB = range(5)
DONE, OWNER, GATHER, SLOT = 0, 3, 6, 9


def wrap(value, size):
    return lax.rem(value, size)


def kernel(items, share, listed, row_hbm, col_hbm, owner_hbm, hidden_hbm, grad_hbm,
           master_hbm, moment1_hbm, moment2_hbm, updated_ref, master, moment1, moment2,
           row_ref, col_ref, owner_ref, size_ref, spots_v, starts_v, spots, starts, hidden, grad, grad_t, to_pair, from_pair, chip, ring_a, ring_b, line, last_a, last_b,
           done_0, done_1, done_2, to_owner, gathered, to_slot, landed,
           sums, sum_in, load_sem, send_sem, recv_sem, move_send, move_recv, sum_send, sum_recv):
    f32, bf16 = jnp.float32, jnp.bfloat16
    d = lax.axis_index("dp")
    z = lax.axis_index("owner")
    x, y, c = lax.div(d, 8), wrap(lax.div(d, 2), 4), wrap(d, 2)

    def device(px, py, pc):
        return {"dp": (px * 4 + py) * 2 + pc}

    partner = device(x, y, 1 - c)

    def near(axis, step):
        if axis == 0:
            return device(wrap(x + step, 4), y, c)
        return device(x, wrap(y + step, 4), c)

    lists = [pltpu.make_async_copy(src, dst, load_sem.at[7 + n]) for n, (src, dst) in enumerate(
        ((owner_hbm, owner_ref), (row_hbm, row_ref), (col_hbm, col_ref)))]
    for copy in lists:
        copy.start()

    barrier = pltpu.get_barrier_semaphore()
    offsets = [(dx, dy) for dx in range(4) for dy in range(4) if dx or dy]
    spread = [device(wrap(x + dx, 4), wrap(y + dy, 4), c) for dx, dy in offsets]
    groups = [[partner], spread, [{"owner": wrap(z + k, N_OWNER)} for k in range(1, N_OWNER)]]
    everyone = sum(groups, [])
    for who in everyone:
        pl.semaphore_signal(barrier, inc=1, device_id=who, device_id_type=MESH)

    def load(src, dst, sem, k):
        columns = pl.ds(pl.multiple_of(k * BLOCK, BLOCK), BLOCK)
        pltpu.make_async_copy(src.at[:, columns], dst.at[k], sem).start()

    def load_grad(k, carry):
        load(grad_hbm, grad, load_sem.at[0], k)
        return carry

    lax.fori_loop(0, grad.shape[0], load_grad, 0, unroll=8)

    def load_hidden(k, carry):
        load(hidden_hbm, hidden, load_sem.at[1], k)
        return carry

    def make_places():
        square = (BLOCK, BLOCK)
        lines = listed // BLOCK
        up_to = lax.broadcasted_iota(jnp.int32, square, 0) <= lax.broadcasted_iota(jnp.int32, square, 1)
        below = lax.broadcasted_iota(jnp.int32, square, 1) < lax.broadcasted_iota(jnp.int32, square, 0)
        for copy in lists:
            copy.wait()
        owners = jnp.concatenate(
            [owner_ref[:, r * BLOCK:(r + 1) * BLOCK] for r in range(lines)]
            + [jnp.full((16 - lines, BLOCK), -1, jnp.int32)], axis=0)
        named = jnp.concatenate([(owners == o).astype(f32) for o in range(N_OWNER)], axis=0)
        named_16 = named.astype(bf16)
        along = jnp.dot(named_16, up_to.astype(f32).astype(bf16), preferred_element_type=f32)
        line_sums = jnp.dot(named_16, jnp.ones(square, bf16), preferred_element_type=f32)
        before = jnp.dot(below.astype(f32).astype(bf16), line_sums.astype(bf16), preferred_element_type=f32)
        spot = jnp.sum((named * (before + along - 1.0)).reshape(N_OWNER, -1, BLOCK), axis=0)
        starts_v[...] = before.reshape(N_OWNER, -1, BLOCK)[:, 0].astype(jnp.int32)
        spot_t = jnp.pad(spot, ((0, BLOCK - spot.shape[0]), (0, 0))).T
        wide = (BLOCK, 2 * BLOCK)
        place = lax.broadcasted_iota(jnp.int32, wide, 1)
        chip_of, pos, chunk = place & (CHIPS - 1), lax.shift_right_logical(place, 4) & 3, lax.shift_right_logical(place, 6)
        wanted = (CHIPS * (24 * pos + CHUNKS * z + chunk) + chip_of).astype(f32)
        which = lax.broadcasted_iota(jnp.int32, (8, BLOCK), 0)
        found = jnp.zeros((8, 2 * BLOCK), f32)
        for r in range(lines):
            hit = jnp.where(spot_t[:, r:r + 1] == wanted, 1.0, 0.0).astype(bf16)
            value = jnp.where(which == 0, row_ref[r:r + 1, :], col_ref[r:r + 1, :]).astype(f32).astype(bf16)
            found = found + jnp.dot(value, hit, preferred_element_type=f32)
        spots_v[...] = found.astype(jnp.int32)
        copies = [pltpu.make_async_copy(spots_v, spots, load_sem.at[2]),
                  pltpu.make_async_copy(starts_v, starts, load_sem.at[3])]
        for copy in copies:
            copy.start()
        for copy in copies:
            copy.wait()

    early = hidden.shape[0] // 2
    lax.fori_loop(0, early, load_hidden, 0, unroll=8)
    make_places()
    pltpu.make_async_copy(grad, grad, load_sem.at[0]).wait()

    def turn(k, carry):
        for n in range(2):
            load(hidden_hbm, hidden, load_sem.at[1], early + 2 * k + n)
        grad_t[k] = grad[k].T
        return carry

    late = hidden.shape[0] - early
    lax.fori_loop(0, late // 2, turn, 0, unroll=4)

    def turn_only(k, carry):
        grad_t[k] = grad[k].T
        return carry

    lax.fori_loop(late // 2, grad.shape[0], turn_only, 0, unroll=4)
    pltpu.make_async_copy(hidden, hidden, load_sem.at[1]).wait()
    states = [pltpu.make_async_copy(src, dst, load_sem.at[4 + n]) for n, (src, dst) in enumerate(
        ((master_hbm, master), (moment1_hbm, moment1), (moment2_hbm, moment2)))]
    for state in states:
        state.start()

    def send(src, dst, item, kind, who):
        pltpu.make_async_remote_copy(
            src_ref=src, dst_ref=dst, send_sem=send_sem.at[kind], recv_sem=recv_sem.at[item, kind],
            device_id=who, device_id_type=MESH).start()

    def take(ref, sem):
        pltpu.make_async_copy(ref, ref, sem).wait()

    def arrive(ref, item, kind):
        take(ref.at[item], recv_sem.at[item, kind])

    def product(place):
        row = jnp.clip(spots[0, place], 0, hidden.shape[0] - 1)
        col = jnp.clip(spots[1, place], 0, grad_t.shape[0] - 1)
        return jnp.dot(grad_t[col], hidden[row], preferred_element_type=f32)

    def slot_of(item, ra, rb, core):
        if item % 2 == 0:
            px, py = wrap(x + ra, 4), wrap(y + rb, 4)
        else:
            px, py = wrap(x + rb, 4), wrap(y + ra, 4)
        return ((item // 2) * 4 + 2 * core + item % 2) * CHIPS + px * 4 + py

    def partner_products(item):
        for j in range(CHIPS):
            to_pair[item, j] = product(slot_of(item, j // 4, j % 4, 1 - c)).astype(bf16)
        if item == int(ORDER[0][1]):
            pl.semaphore_wait(barrier, len(everyone))
        send(to_pair.at[item], from_pair.at[item], item, PAIR, partner)

    def own_products(item):
        arrive(from_pair, item, PAIR)

        for j in range(CHIPS):
            value = product(slot_of(item, j // 4, j % 4, c)) + from_pair[item, j].astype(f32)
            chip[item, j] = value.astype(bf16)

    def ring_start(item):
        axis = item % 2
        send(chip.at[item, pl.ds(8, 2)], ring_a.at[item, 0], item, XA, near(axis, 1))
        send(chip.at[item, pl.ds(10, 2)], ring_a.at[item, 1], item, XA, near(axis, 3))

    def ring_own(item):
        axis = item % 2
        send(chip.at[item, pl.ds(6, 2)], ring_b.at[item, 0, pl.ds(2, 2)], item, XB, near(axis, 1))
        send(chip.at[item, pl.ds(12, 2)], ring_b.at[item, 1, pl.ds(0, 2)], item, XB, near(axis, 3))

    def ring_step(item):
        axis = item % 2
        arrive(ring_a, item, XA)
        chip[item, 4:6] = (chip[item, 4:6].astype(f32) + ring_a[item, 0].astype(f32)).astype(bf16)
        send(chip.at[item, pl.ds(4, 2)], ring_b.at[item, 0, pl.ds(0, 2)], item, XB, near(axis, 1))
        chip[item, 14:16] = (chip[item, 14:16].astype(f32) + ring_a[item, 1].astype(f32)).astype(bf16)
        send(chip.at[item, pl.ds(14, 2)], ring_b.at[item, 1, pl.ds(2, 2)], item, XB, near(axis, 3))

    def ring_end(item):
        axis = 1 - item % 2
        arrive(ring_b, item, XB)
        for rb in (2, 1, 3, 0):
            value = (chip[item, rb].astype(f32) + ring_b[item, 0, rb].astype(f32)
                     + ring_b[item, 1, rb].astype(f32))
            line[item, rb] = value.astype(bf16)
        half = BLOCK // 2
        low, high = pl.ds(0, half), pl.ds(half, half)
        send(line.at[item, 2, low], last_a.at[item, 0], item, YA, near(axis, 1))
        send(line.at[item, 2, high], last_a.at[item, 1], item, YA, near(axis, 3))
        send(line.at[item, 1, high], last_b.at[item, 0, high], item, YB, near(axis, 1))
        send(line.at[item, 3, low], last_b.at[item, 1, low], item, YB, near(axis, 3))

    def line_step(item):
        axis = 1 - item % 2
        half = BLOCK // 2
        low, high = pl.ds(0, half), pl.ds(half, half)
        arrive(last_a, item, YA)
        line[item, 1, :half] = (line[item, 1, :half].astype(f32) + last_a[item, 0].astype(f32)).astype(bf16)
        send(line.at[item, 1, low], last_b.at[item, 0, low], item, YB, near(axis, 1))
        line[item, 3, half:] = (line[item, 3, half:].astype(f32) + last_a[item, 1].astype(f32)).astype(bf16)
        send(line.at[item, 3, high], last_b.at[item, 1, high], item, YB, near(axis, 3))

    def finish(item):
        arrive(last_b, item, YB)
        value = (line[item, 0].astype(f32) + last_b[item, 0].astype(f32) + last_b[item, 1].astype(f32))
        done[item // 2][c * 2 + item % 2] = value.astype(bf16)
        return jnp.sum(value * value, axis=0, keepdims=True)

    done = (done_0, done_1, done_2)
    me_chip = x * 4 + y
    half = BLOCK // 2
    mine = pl.ds(pl.multiple_of(c * half, half), half)

    def move(src, dst, kind, index, who):
        pltpu.make_async_remote_copy(
            src_ref=src, dst_ref=dst, send_sem=move_send.at[kind + index], recv_sem=move_recv.at[kind + index],
            device_id=who, device_id_type=MESH).start()

    def share_done(chunk):
        move(done[chunk].at[pl.ds(2 * c, 2)], done[chunk].at[pl.ds(2 * c, 2)], DONE, chunk, partner)

    def held_for(chunk, owner):
        first = jnp.clip(starts[owner, 0], 0, listed) - me_chip - CHIPS * (CHUNKS * z + chunk) + 383
        pos = jnp.minimum(lax.div(jnp.maximum(first, 0), 384), 3)
        return done[chunk][pos]

    def to_owners(chunk):
        take(done[chunk].at[pl.ds(2 - 2 * c, 2)], move_recv.at[DONE + chunk])
        for j in (1, 2, 0):
            owner = wrap(z + 2 * j + 1 + c, N_OWNER)
            to_owner[chunk, j] = held_for(chunk, owner)
            move(to_owner.at[chunk, j], gathered.at[chunk * 8 + c * 3 + j], OWNER, chunk, {"owner": owner})
        owner = wrap(z + 7, N_OWNER)
        to_owner[chunk, 3] = held_for(chunk, owner)
        move(to_owner.at[chunk, 3, mine], gathered.at[chunk * 8 + 6, mine], OWNER, chunk, {"owner": owner})
        gathered[chunk * 8 + 7] = held_for(chunk, z)

    def share_gathered(chunk):
        take(size_ref, move_recv.at[OWNER + chunk])
        trio = gathered.at[pl.ds(chunk * 8 + c * 3, 3)]
        move(trio, trio, GATHER, chunk, partner)
        rest = gathered.at[chunk * 8 + 6, mine]
        move(rest, rest, GATHER, chunk, partner)

    start = jnp.clip(starts[z, 0], 0, listed)
    count = jnp.where(z == N_OWNER - 1, listed, starts[jnp.minimum(z + 1, N_OWNER - 1), 0]) - start

    def block_for(to_chip):
        first = start + share * (2 * to_chip + c)
        spot = first + ((me_chip - first) & (CHIPS - 1))
        q = jnp.minimum(lax.div(spot, CHIPS), 95)
        chunk = wrap(q, CHUNKS)
        away = (z - lax.div(q, CHUNKS)) & (N_OWNER - 1)
        index = 3 * ((away + 1) & 1) + lax.shift_right_logical(away + 7, 1) - 4
        index = jnp.where(away == 0, 7, jnp.where(away == 7, 6, index))
        return gathered[chunk * 8 + index]

    def to_slots():
        for chunk in range(CHUNKS):
            take(size_ref, move_recv.at[GATHER + chunk])
        for k in sorted(range(len(offsets)), key=lambda k: -sum(min(v, 4 - v) for v in offsets[k])):
            dx, dy = offsets[k]
            to_slot[k] = block_for(wrap(x + dx, 4) * 4 + wrap(y + dy, 4))
            move(to_slot.at[k], landed.at[me_chip], SLOT, 0, spread[k])
        landed[me_chip] = block_for(me_chip)

    def store_slots(total):
        clip = 1.0 / jnp.maximum(jnp.sqrt(jnp.full((BLOCK, BLOCK), total, f32)), 1.0)
        take(to_slot, move_recv.at[SLOT])
        for state in states:
            state.wait()
        for i in range(share):
            slot = d * share + i
            value = landed[(start + slot) & (CHIPS - 1)].astype(f32).T
            scaled = clip * (value * (slot < count).astype(f32))
            first = 0.9 * moment1[i] + 0.1 * scaled
            second = 0.95 * moment2[i] + 0.05 * scaled * scaled
            direction = first * (1.0 / (1.0 - 0.9**10)) / (jnp.sqrt(second * (1.0 / (1.0 - 0.95**10))) + 1e-08)
            updated_ref[i] = master[i] - 0.25 * (direction + 0.1 * master[i])

    def add_start(n, value):
        first = sum(len(group) for group in groups[:n])
        sums[n] = value
        for k, who in enumerate(groups[n]):
            pltpu.make_async_remote_copy(
                src_ref=sums.at[n], dst_ref=sum_in.at[first + k], send_sem=sum_send.at[0],
                recv_sem=sum_recv.at[n], device_id=who, device_id_type=MESH).start()
        return n, first

    def add_end(value, adding):
        n, first = adding
        size = len(groups[n])
        take(sum_in.at[pl.ds(first, size)], sum_recv.at[n])
        for k in range(size):
            value = value + sum_in[first + k]
        return value

    def close(item):
        parts.append(finish(item))

    parts, adding = [], []

    def add_next():
        value = adding[-1][0] if adding else functools.reduce(jnp.add, parts)
        if adding:
            value = add_end(value, adding[-1][1])
        n = len(adding)
        if n < len(groups):
            adding.append((value, add_start(n, value)))
        return value

    stages = {"P": partner_products, "O": own_products, "A": ring_start, "B": ring_own, "R": ring_step, "E": ring_end, "L": line_step,
              "F": close, "s": share_done, "z": to_owners, "g": share_gathered, "a": lambda _: add_next()}
    for name, index in zip("".join(ORDER)[::2], "".join(ORDER)[1::2]):
        stages[name](int(index))
    to_slots()
    total = jnp.sum(add_next())
    store_slots(total)
    for kind, ref in ((PAIR, to_pair), (XA, ring_a), (XB, ring_b), (YA, last_a), (YB, last_b)):
        take(ref, send_sem.at[kind])
    for chunk in range(CHUNKS):
        take(done[chunk].at[pl.ds(0, 2)], move_send.at[DONE + chunk])
        take(size_ref, move_send.at[OWNER + chunk])
        take(size_ref, move_send.at[GATHER + chunk])
    take(to_slot, move_send.at[SLOT])
    take(sum_in, sum_send.at[0])


def step(block_row, block_col, owner_of, hidden, grad_out, master, moment1, moment2):
    share = master.shape[0]
    listed = block_row.shape[0]
    tokens, features = hidden.shape[0], grad_out.shape[1]
    bf16, f32 = jnp.bfloat16, jnp.float32
    items = 2 * CHUNKS
    peers = 1 + CHIPS - 1 + N_OWNER - 1
    block = (BLOCK, BLOCK)
    vmem = pl.BlockSpec(memory_space=pltpu.VMEM)
    hbm = pl.BlockSpec(memory_space=pltpu.HBM)
    return pl.pallas_call(
        functools.partial(kernel, items, share, listed),
        out_shape=jax.ShapeDtypeStruct((share, *block), f32),
        in_specs=[hbm] * 8,
        out_specs=vmem,
        scratch_shapes=[
            pltpu.VMEM((share, *block), f32),
            pltpu.VMEM((share, *block), f32),
            pltpu.VMEM((share, *block), f32),
            pltpu.VMEM((listed // BLOCK, BLOCK), jnp.int32),
            pltpu.VMEM((listed // BLOCK, BLOCK), jnp.int32),
            pltpu.VMEM((1, listed), jnp.int32),
            pltpu.VMEM((7 * BLOCK // 2, BLOCK), bf16),
            pltpu.VMEM((8, 2 * BLOCK), jnp.int32),
            pltpu.VMEM((N_OWNER, BLOCK), jnp.int32),
            pltpu.SMEM((8, 2 * BLOCK), jnp.int32),
            pltpu.SMEM((N_OWNER, BLOCK), jnp.int32),
            pltpu.VMEM((hidden.shape[1] // BLOCK, tokens, BLOCK), bf16),
            pltpu.VMEM((features // BLOCK, tokens, BLOCK), bf16),
            pltpu.VMEM((features // BLOCK, BLOCK, tokens), bf16),
            pltpu.VMEM((items, 16, *block), bf16),
            pltpu.VMEM((items, 16, *block), bf16),
            pltpu.VMEM((items, 16, *block), bf16),
            pltpu.VMEM((items, 2, 2, *block), bf16),
            pltpu.VMEM((items, 2, 4, *block), bf16),
            pltpu.VMEM((items, 4, *block), bf16),
            pltpu.VMEM((items, 2, BLOCK // 2, BLOCK), bf16),
            pltpu.VMEM((items, 2, *block), bf16),
            pltpu.VMEM((4, *block), bf16),
            pltpu.VMEM((4, *block), bf16),
            pltpu.VMEM((4, *block), bf16),
            pltpu.VMEM((CHUNKS, 4, *block), bf16),
            pltpu.VMEM((CHUNKS * N_OWNER, *block), bf16),
            pltpu.VMEM((CHIPS - 1, *block), bf16),
            pltpu.VMEM((CHIPS, *block), bf16),
            pltpu.VMEM((3, 1, BLOCK), f32),
            pltpu.VMEM((peers, 1, BLOCK), f32),
            pltpu.SemaphoreType.DMA((10,)),
            pltpu.SemaphoreType.DMA((5,)),
            pltpu.SemaphoreType.DMA((items, 5)),
            pltpu.SemaphoreType.DMA((10,)),
            pltpu.SemaphoreType.DMA((10,)),
            pltpu.SemaphoreType.DMA((1,)),
            pltpu.SemaphoreType.DMA((3,)),
        ],
        compiler_params=pltpu.CompilerParams(
            collective_id=0, has_side_effects=True, vmem_limit_bytes=36 * 1024 * 1024),
        name="step",
    )(*[pltpu.with_memory_space_constraint(x, pltpu.HBM) for x in (
        block_row.reshape(-1, BLOCK), block_col.reshape(-1, BLOCK), owner_of.T, hidden, grad_out,
        master, moment1, moment2)])


def on_device(hidden, grad_out, block_row, block_col, owner_of, master, moment1, moment2):
    updated = step(block_row, block_col, owner_of, hidden, grad_out, master[0], moment1[0], moment2[0])
    return updated[None]


def solution(mesh):
    placed = (
        P("dp", None),
        P("dp", None),
        P(),
        P(),
        P(),
        P("owner", "dp", None, None),
        P("owner", "dp", None, None),
        P("owner", "dp", None, None),
    )
    return jax.shard_map(
        on_device,
        mesh=mesh,
        in_specs=placed,
        out_specs=P("owner", "dp", None, None),
        check_vma=False,
    )
```

time: 64 us -> 55.8 us (0.87)
  Pallas kernels: 58.8 us -> 54.8 us
  other arithmetic: 3.7 us -> 0 us
  between operations: 0.66 us -> 0.01 us
    pallas_call x1, Pallas kernels: 58.8 us -> 54.8 us  [step(): pl.pallas_call(functools.partial(kernel, items, share, listed), out_shape...]
    sub x1 -> x0, other arithmetic: 2.87 us -> none  [on_device(): return master - 0.25 * (direction + 0.1 * master)]
    unnamed x4 -> x1, local copies, waits for them, and re-layouts: 0.01 us -> 0.88 us
    unnamed x1 -> x0, other arithmetic: 0.83 us -> none
where the time goes in v5:
time: 55.8 us; the launch traced here: 55.6 us
  Pallas kernels  54.8 us (98%)
  local copies, waits for them, and re-layouts  0.88 us (2%)
    pallas_call x1, Pallas kernels, step(): pl.pallas_call(functools.partial(kernel, items, share, listed), out_shape...  54.8 us

profile of v5, /device:TPU:1, one launch (start us, length us, event | category | flops | bytes accessed | tf_op | source)
XLA Modules:
  0.0 55.6 jit_solution(5900079594543584651)
XLA Ops:
  0.0 54.8 %step.1 = f32[12,128,128]{2,1,0:T(8,128)S(1)} custom-call(s32[12,128]{1,0:T(8,128)} %bitcast.11, s32[12,128]{1,0:T(8,128)} %bitcast.12, s32[1,1536]{1,0:T(1,128)} %bitcast.13, bf16[256,14336]{1,0:T(8,128)(2,1)} %hidden_hbm.1, bf16[256,4096]{1,0:T(8,128)(2,1)} %grad_hbm.1, f32[12,128,128]{2,1,0:T(8,128)} %bitcast.8, f32[12,128,128]{2,1,0:T(8,128)} %bitcast.9, ...), custom_call_target="tpu_custom_call" | custom-call | tf_op jit(solution)/shard_map/step/pallas_call | solution.py:350
  54.8 0.9 %copy.10 = f32[1,12,128,128]{3,2,1,0:T(8,128)} copy(f32[1,12,128,128]{3,2,1,0:T(8,128)S(1)} %bitcast.7) | data formatting | bytes 1572864

commit v6 on v5

--- a/solution.py
+++ b/solution.py
@@ -12,11 +12,11 @@
 MESH = pl.DeviceIdType.MESH
 CHUNKS = 3
 ORDER = (
-    "P2P3P5P4O2A2O3A3B2P0B3O4A4O5A5P1R2R3B5O0A0B4R4R5O1E2E3A1B1R0",
-    "E5E4L3B0L2R1L5L4F3F2s1E0E1F5F4s2z1L0L1z2F0F1s0a0z0a0g2g1a0g0",
+    "P5P4P3P2O5B5O4A4P1B4A5P0O3A3O2A2B3R4O0R5O1A0B2A1R3R2E4",
+    "E5B0R1R0B1E2E3F4F5s2E1E0z2F2F3s1z1F1F0s0a0z0a0g2g1a0g0",
 )
 CHIPS = 16
-PAIR, XA, XB, YA, YB = range(5)
+PAIR, XA, XB, YA = range(4)
 DONE, OWNER, GATHER, SLOT = 0, 3, 6, 9
 
 
@@ -26,7 +26,7 @@
 
 def kernel(items, share, listed, row_hbm, col_hbm, owner_hbm, hidden_hbm, grad_hbm,
            master_hbm, moment1_hbm, moment2_hbm, updated_ref, master, moment1, moment2,
-           row_ref, col_ref, owner_ref, size_ref, spots_v, starts_v, spots, starts, hidden, grad, grad_t, to_pair, from_pair, chip, ring_a, ring_b, line, last_a, last_b,
+           row_ref, col_ref, owner_ref, size_ref, spots_v, starts_v, spots, starts, hidden, grad, grad_t, to_pair, from_pair, chip, ring_a, ring_b, line, last,
            done_0, done_1, done_2, to_owner, gathered, to_slot, landed,
            sums, sum_in, load_sem, send_sem, recv_sem, move_send, move_recv, sum_send, sum_recv):
     f32, bf16 = jnp.float32, jnp.bfloat16
@@ -194,27 +194,15 @@
             value = (chip[item, rb].astype(f32) + ring_b[item, 0, rb].astype(f32)
                      + ring_b[item, 1, rb].astype(f32))
             line[item, rb] = value.astype(bf16)
-        half = BLOCK // 2
-        low, high = pl.ds(0, half), pl.ds(half, half)
-        send(line.at[item, 2, low], last_a.at[item, 0], item, YA, near(axis, 1))
-        send(line.at[item, 2, high], last_a.at[item, 1], item, YA, near(axis, 3))
-        send(line.at[item, 1, high], last_b.at[item, 0, high], item, YB, near(axis, 1))
-        send(line.at[item, 3, low], last_b.at[item, 1, low], item, YB, near(axis, 3))
-
-    def line_step(item):
-        axis = 1 - item % 2
-        half = BLOCK // 2
-        low, high = pl.ds(0, half), pl.ds(half, half)
-        arrive(last_a, item, YA)
-        line[item, 1, :half] = (line[item, 1, :half].astype(f32) + last_a[item, 0].astype(f32)).astype(bf16)
-        send(line.at[item, 1, low], last_b.at[item, 0, low], item, YB, near(axis, 1))
-        line[item, 3, half:] = (line[item, 3, half:].astype(f32) + last_a[item, 1].astype(f32)).astype(bf16)
-        send(line.at[item, 3, high], last_b.at[item, 1, high], item, YB, near(axis, 3))
+        for step in (2, 1, 3):
+            send(line.at[item, step], last.at[item, step - 1], item, YA, near(axis, step))
 
     def finish(item):
-        arrive(last_b, item, YB)
-        value = (line[item, 0].astype(f32) + last_b[item, 0].astype(f32) + last_b[item, 1].astype(f32))
-        done[item // 2][c * 2 + item % 2] = value.astype(bf16)
+        arrive(last, item, YA)
+        value = line[item, 0].astype(f32)
+        for k in range(3):
+            value = value + last[item, k].astype(f32)
+        done[item // 2][c * 2 + item % 2] = value.T.astype(bf16)
         return jnp.sum(value * value, axis=0, keepdims=True)
 
     done = (done_0, done_1, done_2)
@@ -275,19 +263,25 @@
             move(to_slot.at[k], landed.at[me_chip], SLOT, 0, spread[k])
         landed[me_chip] = block_for(me_chip)
 
+    def decay_states():
+        for state in states:
+            state.wait()
+        for i in range(share):
+            master[i] = (1.0 - 0.25 * 0.1) * master[i]
+            moment1[i] = 0.9 * moment1[i]
+            moment2[i] = 0.95 * moment2[i]
+
     def store_slots(total):
         clip = 1.0 / jnp.maximum(jnp.sqrt(jnp.full((BLOCK, BLOCK), total, f32)), 1.0)
         take(to_slot, move_recv.at[SLOT])
-        for state in states:
-            state.wait()
         for i in range(share):
             slot = d * share + i
-            value = landed[(start + slot) & (CHIPS - 1)].astype(f32).T
+            value = landed[(start + slot) & (CHIPS - 1)].astype(f32)
             scaled = clip * (value * (slot < count).astype(f32))
-            first = 0.9 * moment1[i] + 0.1 * scaled
-            second = 0.95 * moment2[i] + 0.05 * scaled * scaled
-            direction = first * (1.0 / (1.0 - 0.9**10)) / (jnp.sqrt(second * (1.0 / (1.0 - 0.95**10))) + 1e-08)
-            updated_ref[i] = master[i] - 0.25 * (direction + 0.1 * master[i])
+            first = moment1[i] + 0.1 * scaled
+            second = moment2[i] + 0.05 * scaled * scaled
+            root = jnp.sqrt(second * (1.0 / (1.0 - 0.95**10))) + 1e-08
+            updated_ref[i] = master[i] - first * (0.25 / (1.0 - 0.9**10)) / root
 
     def add_start(n, value):
         first = sum(len(group) for group in groups[:n])
@@ -320,14 +314,15 @@
             adding.append((value, add_start(n, value)))
         return value
 
-    stages = {"P": partner_products, "O": own_products, "A": ring_start, "B": ring_own, "R": ring_step, "E": ring_end, "L": line_step,
+    stages = {"P": partner_products, "O": own_products, "A": ring_start, "B": ring_own, "R": ring_step, "E": ring_end,
               "F": close, "s": share_done, "z": to_owners, "g": share_gathered, "a": lambda _: add_next()}
     for name, index in zip("".join(ORDER)[::2], "".join(ORDER)[1::2]):
         stages[name](int(index))
     to_slots()
+    decay_states()
     total = jnp.sum(add_next())
     store_slots(total)
-    for kind, ref in ((PAIR, to_pair), (XA, ring_a), (XB, ring_b), (YA, last_a), (YB, last_b)):
+    for kind, ref in ((PAIR, to_pair), (XA, ring_a), (XB, ring_b), (YA, last)):
         take(ref, send_sem.at[kind])
     for chunk in range(CHUNKS):
         take(done[chunk].at[pl.ds(0, 2)], move_send.at[DONE + chunk])
@@ -373,8 +368,7 @@
             pltpu.VMEM((items, 2, 2, *block), bf16),
             pltpu.VMEM((items, 2, 4, *block), bf16),
             pltpu.VMEM((items, 4, *block), bf16),
-            pltpu.VMEM((items, 2, BLOCK // 2, BLOCK), bf16),
-            pltpu.VMEM((items, 2, *block), bf16),
+            pltpu.VMEM((items, 3, *block), bf16),
             pltpu.VMEM((4, *block), bf16),
             pltpu.VMEM((4, *block), bf16),
             pltpu.VMEM((4, *block), bf16),
@@ -385,8 +379,8 @@
             pltpu.VMEM((3, 1, BLOCK), f32),
             pltpu.VMEM((peers, 1, BLOCK), f32),
             pltpu.SemaphoreType.DMA((10,)),
-            pltpu.SemaphoreType.DMA((5,)),
-            pltpu.SemaphoreType.DMA((items, 5)),
+            pltpu.SemaphoreType.DMA((4,)),
+            pltpu.SemaphoreType.DMA((items, 4)),
             pltpu.SemaphoreType.DMA((10,)),
             pltpu.SemaphoreType.DMA((10,)),
             pltpu.SemaphoreType.DMA((1,)),

time: 55.8 us -> 54.1 us (0.970)
  Pallas kernels: 54.8 us -> 53.1 us
    pallas_call x1, Pallas kernels: 54.8 us -> 53.1 us  [step(): pl.pallas_call(functools.partial(kernel, items, share, listed), out_shape...]
where the time goes in v6:
time: 54.1 us; the launch traced here: 54 us
  Pallas kernels  53.1 us (98%)
  local copies, waits for them, and re-layouts  0.88 us (2%)
    pallas_call x1, Pallas kernels, step(): pl.pallas_call(functools.partial(kernel, items, share, listed), out_shape...  53.1 us

profile of v6, /device:TPU:1, one launch (start us, length us, event | category | flops | bytes accessed | tf_op | source)
XLA Modules:
  0.0 54.0 jit_solution(8248392754495214066)
XLA Ops:
  0.0 53.1 %step.1 = f32[12,128,128]{2,1,0:T(8,128)S(1)} custom-call(s32[12,128]{1,0:T(8,128)} %bitcast.11, s32[12,128]{1,0:T(8,128)} %bitcast.12, s32[1,1536]{1,0:T(1,128)} %bitcast.13, bf16[256,14336]{1,0:T(8,128)(2,1)} %hidden_hbm.1, bf16[256,4096]{1,0:T(8,128)(2,1)} %grad_hbm.1, f32[12,128,128]{2,1,0:T(8,128)} %bitcast.8, f32[12,128,128]{2,1,0:T(8,128)} %bitcast.9, ...), custom_call_target="tpu_custom_call" | custom-call | tf_op jit(solution)/shard_map/step/pallas_call | solution.py:345
  53.1 0.9 %copy.10 = f32[1,12,128,128]{3,2,1,0:T(8,128)} copy(f32[1,12,128,128]{3,2,1,0:T(8,128)S(1)} %bitcast.7) | data formatting | bytes 1572864

commit v7 on v6

--- a/solution.py
+++ b/solution.py
@@ -12,8 +12,8 @@
 MESH = pl.DeviceIdType.MESH
 CHUNKS = 3
 ORDER = (
-    "P5P4P3P2O5B5O4A4P1B4A5P0O3A3O2A2B3R4O0R5O1A0B2A1R3R2E4",
-    "E5B0R1R0B1E2E3F4F5s2E1E0z2F2F3s1z1F1F0s0a0z0a0g2g1a0g0",
+    "P0P1P5P2P4O0A0B0O1A1B1O5P3A5O4O2A2R0A4R1O3A3B3R2E1B2E0",
+    "R3B4R5B5R4E2E3F0F1s0z0E4E5F3F2s1z1F5F4s2a0z2a0g0g1a0g2",
 )
 CHIPS = 16
 PAIR, XA, XB, YA = range(4)

time: 54.1 us -> 53.3 us (0.985)
  Pallas kernels: 53.1 us -> 52.2 us
    pallas_call x1, Pallas kernels: 53.1 us -> 52.2 us  [step(): pl.pallas_call(functools.partial(kernel, items, share, listed), out_shape...]
where the time goes in v7:
time: 53.3 us; the launch traced here: 53.1 us
  Pallas kernels  52.2 us (98%)
  local copies, waits for them, and re-layouts  0.88 us (2%)
    pallas_call x1, Pallas kernels, step(): pl.pallas_call(functools.partial(kernel, items, share, listed), out_shape...  52.2 us

profile of v7, /device:TPU:1, one launch (start us, length us, event | category | flops | bytes accessed | tf_op | source)
XLA Modules:
  0.0 53.1 jit_solution(10879469318297218287)
XLA Ops:
  0.0 52.2 %step.1 = f32[12,128,128]{2,1,0:T(8,128)S(1)} custom-call(s32[12,128]{1,0:T(8,128)} %bitcast.11, s32[12,128]{1,0:T(8,128)} %bitcast.12, s32[1,1536]{1,0:T(1,128)} %bitcast.13, bf16[256,14336]{1,0:T(8,128)(2,1)} %hidden_hbm.1, bf16[256,4096]{1,0:T(8,128)(2,1)} %grad_hbm.1, f32[12,128,128]{2,1,0:T(8,128)} %bitcast.8, f32[12,128,128]{2,1,0:T(8,128)} %bitcast.9, ...), custom_call_target="tpu_custom_call" | custom-call | tf_op jit(solution)/shard_map/step/pallas_call | solution.py:345
  52.3 0.9 %copy.10 = f32[1,12,128,128]{3,2,1,0:T(8,128)} copy(f32[1,12,128,128]{3,2,1,0:T(8,128)S(1)} %bitcast.7) | data formatting | bytes 1572864

commit v8 on v7

--- a/solution.py
+++ b/solution.py
@@ -12,7 +12,7 @@
 MESH = pl.DeviceIdType.MESH
 CHUNKS = 3
 ORDER = (
-    "P0P1P5P2P4O0A0B0O1A1B1O5P3A5O4O2A2R0A4R1O3A3B3R2E1B2E0",
+    "P0P1P5P2P4O0O1O5P3A5O4O2A2R0A4R1O3A3B3R2E1B2E0",
     "R3B4R5B5R4E2E3F0F1s0z0E4E5F3F2s1z1F5F4s2a0z2a0g0g1a0g2",
 )
 CHIPS = 16
@@ -165,9 +165,13 @@
     def own_products(item):
         arrive(from_pair, item, PAIR)
 
-        for j in range(CHIPS):
+        for n, j in enumerate((8, 9, 10, 11, 6, 7, 12, 13, 4, 5, 14, 15, 0, 1, 2, 3)):
             value = product(slot_of(item, j // 4, j % 4, c)) + from_pair[item, j].astype(f32)
             chip[item, j] = value.astype(bf16)
+            if item < 2 and n == 3:
+                ring_start(item)
+            if item < 2 and n == 7:
+                ring_own(item)
 
     def ring_start(item):
         axis = item % 2

time: 53.3 us -> 53.6 us (level)
  no operation moved by 1% of the time
where the time goes in v8:
time: 53.6 us; the launch traced here: 53.5 us
  Pallas kernels  52.6 us (98%)
  local copies, waits for them, and re-layouts  0.88 us (2%)
    pallas_call x1, Pallas kernels, step(): pl.pallas_call(functools.partial(kernel, items, share, listed), out_shape...  52.6 us

profile of v8, /device:TPU:1, one launch (start us, length us, event | category | flops | bytes accessed | tf_op | source)
XLA Modules:
  0.0 53.5 jit_solution(12048630716467481531)
XLA Ops:
  0.0 52.6 %step.1 = f32[12,128,128]{2,1,0:T(8,128)S(1)} custom-call(s32[12,128]{1,0:T(8,128)} %bitcast.11, s32[12,128]{1,0:T(8,128)} %bitcast.12, s32[1,1536]{1,0:T(1,128)} %bitcast.13, bf16[256,14336]{1,0:T(8,128)(2,1)} %hidden_hbm.1, bf16[256,4096]{1,0:T(8,128)(2,1)} %grad_hbm.1, f32[12,128,128]{2,1,0:T(8,128)} %bitcast.8, f32[12,128,128]{2,1,0:T(8,128)} %bitcast.9, ...), custom_call_target="tpu_custom_call" | custom-call | tf_op jit(solution)/shard_map/step/pallas_call | solution.py:349
  52.6 0.9 %copy.10 = f32[1,12,128,128]{3,2,1,0:T(8,128)} copy(f32[1,12,128,128]{3,2,1,0:T(8,128)S(1)} %bitcast.7) | data formatting | bytes 1572864
